TPU v7x, 256 devices: a whole 4x4x8 slice. The times are simulated.
256 devices in a mesh: pair: 64 (over y, z, core), aux: 4 (over x).
Axes of the slice: x: 4, y: 4, z: 8, core: 2. Of those that a mesh axis runs over, the one named last changes fastest.
Arguments:
- factors: bfloat16 [64, 8192, 8, 128], P('pair', 'aux'), may hold values from -0.0625 to 0.0625
- amplitudes: bfloat16 [3072, 128, 128], P('pair'), may hold values from -6 to 6
- block_list: int32 [3072, 3], P('pair'), may hold values from 0 to 63, as said below
- owner_map: int32 [64], replicated, may hold values from 0 to 63, as said below
Outputs:
- residual_blocks: bfloat16 [3072, 128, 128], P('pair')
Inputs may be any that keep to these rules, and one draw needn't show every extreme that they name: `block_list`: each row (k, A, C) names an occupied orbital below 64 and two virtual blocks below 8; no row repeats. Among the 48 rows of one device at most 2 have orbitals with the same owner_map entry, and exactly 2 for some entry on every device. `owner_map`: A permutation: entry k is the row of factors that holds orbital k.
All inputs are finite; a program needn't handle non-finite values.
Results may differ from a plain program's by a relative error of at most 0.0046.
Values may be sent and summed in bfloat16 or wider, within the bound.
A program may use at most 64 MiB of HBM per device.

v0:
```python
import jax
import jax.numpy as jnp
from jax import lax
from jax.sharding import PartitionSpec as P

CAP = 2


def on_device(factors, amplitudes, block_list, owner_map):
    pair_count = lax.axis_size("pair")
    slot_total = pair_count * CAP
    block_count = amplitudes.shape[0]
    block_width = amplitudes.shape[1]
    virt_blocks = factors.shape[2]
    share_rows = factors.shape[1]
    orbital_total = owner_map.shape[0]
    orbitals = block_list[:, 0]
    block_a = block_list[:, 1]
    block_c = block_list[:, 2]
    matches = orbitals[:, None] == lax.iota(jnp.int32, orbital_total)[None, :]
    owners = jnp.sum(jnp.where(matches, owner_map[None, :], 0), axis=1)
    owner_hits = (owners[:, None] == lax.iota(jnp.int32, pair_count)[None, :]).astype(jnp.int32)
    earlier = jnp.cumsum(owner_hits, axis=0) - owner_hits
    slot_rank = jnp.sum(earlier * owner_hits, axis=1)
    slots = owners * CAP + slot_rank
    placing = slots[:, None] == lax.iota(jnp.int32, slot_total)[None, :]
    place_matrix = placing.astype(jnp.bfloat16)
    flat_blocks = amplitudes.reshape(block_count, block_width * block_width)
    send_blocks = jnp.einsum(
        "js,jm->sm", place_matrix, flat_blocks, preferred_element_type=jnp.float32
    )
    send_blocks = send_blocks.astype(jnp.bfloat16).reshape(
        pair_count, CAP, block_width, block_width
    )
    send_a = jnp.sum(jnp.where(placing, block_a[:, None] + 1, 0), axis=0)
    send_c = jnp.sum(jnp.where(placing, block_c[:, None] + 1, 0), axis=0)
    send_index = (
        jnp.stack([send_a, send_c], axis=-1).astype(jnp.bfloat16).reshape(pair_count, CAP, 2)
    )
    recv_blocks, recv_index = (
        lax.all_to_all(send_blocks, "pair", split_axis=0, concat_axis=0, tiled=True),
        lax.all_to_all(send_index, "pair", split_axis=0, concat_axis=0, tiled=True),
    )
    recv_index = recv_index.reshape(slot_total, 2).astype(jnp.int32) - 1
    slot_a = recv_index[:, 0]
    slot_c = recv_index[:, 1]
    onehot_a = (slot_a[:, None] == lax.iota(jnp.int32, virt_blocks)[None, :]).astype(jnp.bfloat16)
    onehot_c = (slot_c[:, None] == lax.iota(jnp.int32, virt_blocks)[None, :]).astype(jnp.bfloat16)
    combined = (onehot_c[:, :, None] * onehot_a[:, None, :]).reshape(
        slot_total, virt_blocks * virt_blocks
    )
    recv_flat = recv_blocks.reshape(slot_total, block_width * block_width)
    weights = jnp.einsum("sm,sn->mn", combined, recv_flat, preferred_element_type=jnp.float32)
    weights = weights.reshape(virt_blocks, virt_blocks, block_width, block_width)
    weights = jnp.transpose(weights, (0, 3, 1, 2)).reshape(
        virt_blocks * block_width, virt_blocks * block_width
    )
    weights = weights.astype(jnp.bfloat16)
    factor_flat = factors.reshape(share_rows, virt_blocks * block_width)
    factor_rows = factor_flat
    inter_share = lax.psum_scatter(
        jnp.dot(factor_rows, weights, preferred_element_type=jnp.float32),
        "pair",
        scatter_dimension=0,
        tiled=True,
    )
    inter_share = inter_share.astype(jnp.bfloat16)
    shard_rows = lax.all_gather(inter_share, "pair", axis=0, tiled=True)
    height = shard_rows.shape[0]
    factor_rows = factor_flat
    left = shard_rows.reshape(height, virt_blocks, block_width)
    right = factor_rows.reshape(height, virt_blocks, block_width)
    projected = jnp.einsum("qAa,qCc->ACac", left, right, preferred_element_type=jnp.float32)
    safe_a = jnp.maximum(slot_a, 0)
    safe_c = jnp.maximum(slot_c, 0)
    summed = lax.psum(projected, "aux")
    picked = summed[safe_a, safe_c].astype(jnp.bfloat16)
    picked = picked.reshape(pair_count, CAP, block_width, block_width)
    returned = lax.all_to_all(picked, "pair", split_axis=0, concat_axis=0, tiled=True)
    returned = returned.reshape(slot_total, block_width * block_width)
    result = jnp.einsum("js,sm->jm", place_matrix, returned, preferred_element_type=jnp.float32)
    return result.astype(jnp.bfloat16).reshape(block_count, block_width, block_width)


def solution(mesh):
    placed = (P("pair", "aux", None, None), P("pair", None, None), P("pair", None), P())
    return jax.shard_map(
        on_device, mesh=mesh, in_specs=placed, out_specs=P("pair", None, None), check_vma=False
    )
```

profile of v0, /device:TPU:1, one launch (start us, length us, event | category | flops | bytes accessed | tf_op | source)
XLA Modules:
  0.0 617.8 jit_solution(2545537378293932037)
XLA Ops:
  6.5 0.8 add_bitcast_fusion
  7.3 0.8 select_reduce_fusion.3
  8.2 0.1 fusion.18
  8.2 0.1 reduce_window_sum.11
  8.3 0.2 select_reduce_fusion.2
  8.5 0.1 select_reduce_fusion.1
  8.7 0.1 stack.10
  8.8 0.2 stack.9
  9.0 0.7 copy.26
  9.6 13.2 %all-to-all-start = ((bf16[64,2,2]{1,2,0:T(2,128)(2,1)}), bf16[64,2,2]{1,2,0:T(2,128)(2,1)S(1)}, u32[]{:S(2)}, u32[]{:S(2)}) async-start(bf16[64,2,2]{1,2,0:T(2,128)(2,1)} %copy.26), calls=%async_computation | async-start | bytes 65536 | tf_op jit(solution)/shard_map/all_to_all | solution.py:42
  22.8 2.8 fusion.10
  25.6 3.2 copy.39
  28.8 3.2 all-to-all-done
  32.0 7.3 %all-to-all-start.1 = ((bf16[64,2,128,128]{3,2,1,0:T(8,128)(2,1)}), bf16[64,2,128,128]{3,2,1,0:T(8,128)(2,1)}, u32[]{:S(2)}, u32[]{:S(2)}) async-start(bf16[64,2,128,128]{3,2,1,0:T(8,128)(2,1)} %bitcast.84), calls=%async_computation.1 | async-start | bytes 8388608 | tf_op jit(solution)/shard_map/all_to_all | solution.py:41
  39.3 0.2 reduce-scatter.4.cloned.1.call-start
  39.6 0.1 copy.27
  39.7 0.1 copy.28
  39.8 0.1 sub.11
  40.0 95.3 %all-to-all-done.1 = bf16[64,2,128,128]{3,2,1,0:T(8,128)(2,1)} async-done(((bf16[64,2,128,128]{3,2,1,0:T(8,128)(2,1)}), bf16[64,2,128,128]{3,2,1,0:T(8,128)(2,1)}, u32[]{:S(2)}, u32[]{:S(2)}) %all-to-all-start.1) | async-done | bytes 4194336 | tf_op jit(solution)/shard_map/all_to_all | solution.py:41
  135.2 7.7 %copy.70 = bf16[16,8,128,128]{3,1,2,0:T(8,128)(2,1)} copy(bf16[16,8,128,128]{3,2,1,0:T(8,128)(2,1)} %bitcast.39) | data formatting | bytes 8388608
  142.9 6.4 %copy.29 = bf16[128,16384]{0,1:T(8,128)(2,1)} copy(bf16[128,16384]{1,0:T(8,128)(2,1)} %bitcast.88) | data formatting | bytes 8388608 | tf_op jit(solution)/shard_map/reshape | solution.py:52
  149.3 3.8 convert_bitcast_fusion
  153.1 3.3 copy.30
  156.3 10.6 %convolution_bitcast_fusion = f32[2048,1024]{0,1:T(8,128)} fusion(bf16[256,8,8,128]{3,2,1,0:T(8,128)(2,1)} %bitcast.92, bf16[128,8,8,128]{3,2,1,0:T(8,128)(2,1)} %bitcast.90), kind=kOutput, calls=%fused_computation.3 | convolution fusion | flops 4294967296 | bytes 14680064 | tf_op jit(solution)/shard_map/dot_general | solution.py:62
  166.9 9.3 %copy.36 = f32[2048,1024]{1,0:T(8,128)} copy(f32[2048,1024]{0,1:T(8,128)} %convolution_bitcast_fusion) | data formatting | bytes 16777216
  176.2 0.0 reduce-scatter.4.cloned.1.call-update
  176.2 0.3 all-gather.2.cloned.1.call-start
  176.5 143.6 %reduce-scatter.4.cloned.1.call-done = f32[32,1024]{1,0:T(8,128)} async-done(((f32[2048,1024]{1,0:T(8,128)}), f32[32,1024]{1,0:T(8,128)}) %reduce-scatter.4.cloned.1.call-update) | async-done | bytes 131088 | tf_op jit(solution)/shard_map/reduce_scatter | solution.py:61
  320.2 1.5 convert_element_type.57
  321.7 0.0 all-gather.2.cloned.1.call-update
  321.7 83.6 %all-gather.2.cloned.1.call-done = bf16[2048,1024]{1,0:T(8,128)(2,1)} async-done(((bf16[32,1024]{1,0:T(8,128)(2,1)}), bf16[2048,1024]{1,0:T(8,128)(2,1)}) %all-gather.2.cloned.1.call-update) | async-done | bytes 4194320 | tf_op jit(solution)/shard_map/all_gather | solution.py:68
  405.3 6.5 %copy.32 = bf16[2048,1024]{0,1:T(8,128)(2,1)} copy(bf16[2048,1024]{1,0:T(8,128)(2,1)} %all-gather.2.cloned.1.call-done) | data formatting | bytes 8388608 | tf_op jit(solution)/shard_map/all_gather | solution.py:68
  411.8 9.9 %fusion.7 = f32[8,8,128,128]{3,2,1,0:T(8,128)} fusion(bf16[2048,8,128,1]{0,2,3,1:T(8,128)(2,1)} %bitcast.89, bf16[2048,8,128]{2,1,0:T(8,128)(2,1)} %bitcast.93), kind=kOutput, calls=%fused_computation.12 | convolution fusion | flops 4294967296 | bytes 12582912 | tf_op jit(solution)/shard_map/qAa,qCc->ACac/dot_general | solution.py:73
  421.7 78.1 %all-reduce.1 = bf16[8,8,128,128]{3,2,1,0:T(8,128)(2,1)S(1)} all-reduce(f32[8,8,128,128]{3,2,1,0:T(8,128)} %fusion.7), channel_id=1, replica_groups=mesh['pair'=64,'aux'=4] {'aux'}, use_global_device_ids=true, to_apply=%region_6.7 | all-reduce | flops 1048576 | bytes 6291456 | tf_op jit(solution)/shard_map/psum | solution.py:76
  499.8 3.1 gather_fusion
  502.8 103.9 %all_to_all.15 = bf16[64,2,128,128]{3,2,1,0:T(8,128)(2,1)S(1)} all-to-all(bf16[64,2,128,128]{3,2,1,0:T(8,128)(2,1)} %bitcast.86), channel_id=1, replica_groups=mesh['pair'=64,'aux'=4] {'pair'}, dimensions={0} | all-to-all | bytes 8388608 | tf_op jit(solution)/shard_map/all_to_all | solution.py:79
  606.7 2.7 fusion.15
  609.4 1.6 copy.44
  (7 shorter events, 0.1 us)
Async XLA Ops:
  9.6 22.4 %all-to-all-start = ((bf16[64,2,2]{1,2,0:T(2,128)(2,1)}), bf16[64,2,2]{1,2,0:T(2,128)(2,1)S(1)}, u32[]{:S(2)}, u32[]{:S(2)}) async-start(bf16[64,2,2]{1,2,0:T(2,128)(2,1)} %copy.26), calls=%async_computation | async-start | bytes 65536 | tf_op jit(solution)/shard_map/all_to_all | solution.py:42
  32.0 103.2 %all-to-all-start.1 = ((bf16[64,2,128,128]{3,2,1,0:T(8,128)(2,1)}), bf16[64,2,128,128]{3,2,1,0:T(8,128)(2,1)}, u32[]{:S(2)}, u32[]{:S(2)}) async-start(bf16[64,2,128,128]{3,2,1,0:T(8,128)(2,1)} %bitcast.84), calls=%async_computation.1 | async-start | bytes 8388608 | tf_op jit(solution)/shard_map/all_to_all | solution.py:41
  39.3 280.8 %reduce-scatter.4.cloned.1.call-start = ((), (), s32[]{:S(2)}) async-start(), calls=%async_computation.5 | async-start | bytes 8519680 | tf_op jit(solution)/shard_map/reduce_scatter | solution.py:61
  176.2 229.1 %all-gather.2.cloned.1.call-start = ((), (), s32[]{:S(2)}) async-start(), calls=%async_computation.4 | async-start | bytes 4259840 | tf_op jit(solution)/shard_map/all_gather | solution.py:68
Sparse Core Ops, SparseCore 0:
  176.4 143.7 reduce-scatter.3
  323.3 81.9 all-gather.1
where the time goes:
time: 619 us; the launch traced here: 618 us
  waiting for transfers between devices  326 us (53%)
  blocking collectives  182 us (29%)
  local copies, waits for them, and re-layouts  42.2 us (7%)
  matrix products  29.8 us (5%)
  starting transfers between devices  21 us (3%)
  between operations  13.5 us (2%)
    reduce_scatter x1, waiting for transfers between devices, on_device(): lax.psum_scatter(jnp.dot(factor_rows, weights, preferred_element_type=jnp...  144 us
    all_to_all x1, blocking collectives, on_device(): lax.all_to_all(picked, 'pair', split_axis=0, concat_axis=0, tiled=True)  104 us
    all_to_all x1, waiting for transfers between devices, on_device(): lax.all_to_all(send_blocks, 'pair', split_axis=0, concat_axis=0, tiled=True)  95.3 us
    all_gather x1, waiting for transfers between devices, on_device(): shard_rows = lax.all_gather(inter_share, 'pair', axis=0, tiled=True)  83.6 us
    psum x1, blocking collectives, on_device(): summed = lax.psum(projected, 'aux')  78.1 us
    unnamed x4, local copies, waits for them, and re-layouts  21.7 us
    all_to_all x1, starting transfers between devices, on_device(): lax.all_to_all(send_index, 'pair', split_axis=0, concat_axis=0, tiled=True)  13.2 us
  transfers between devices with their start and end apart: 4, of which 4 were waited for; matrix products, arithmetic and copies ran while one was open for 1% of the time, Pallas kernels for 0%

commit v1 on v0

v1 whole, which is shorter than its diff:
```python
import functools

import jax
import jax.numpy as jnp
from jax import lax
from jax.experimental import pallas as pl
from jax.experimental.pallas import tpu as pltpu
from jax.sharding import PartitionSpec as P

CAP = 2
NY = 4
F32 = jnp.float32
BF16 = jnp.bfloat16
MESH = pl.DeviceIdType.MESH
NT = (((1,), (1,)), ((), ()))


def middle_kernel(
    nz, nx, f_ref, w_ref, out_ref, wall, sibtx, sibrx, part, ytx1, yrx1, ytx2, yrx2, ztx, zrx, xt,
    ptx, prx, relay, acc, s_w, r_w, s_sib, r_sib, s_y1, r_y1, s_y2, r_y2, s_z, r_z, s_gz, r_gz,
    s_gy, r_gy, s_gs, r_gs, s_p, r_p,
):
    pair, aux = lax.axis_index("pair"), lax.axis_index("aux")
    core, z, y = lax.rem(pair, 2), lax.rem(pair // 2, nz), pair // (2 * nz)
    half = sibtx.shape[2]
    seg = half // nz
    mid = half // 2
    cols = part.shape[3]
    rows = 2 * half

    def at(y_, z_, c_):
        return {"pair": (lax.rem(y_ + NY, NY) * nz + lax.rem(z_ + nz, nz)) * 2 + c_}

    sib = at(y, z, 1 - core)
    up, down = at(y + 1, z, core), at(y - 1, z, core)
    right, left = {"aux": lax.rem(aux + 1, nx)}, {"aux": lax.rem(aux + nx - 1, nx)}

    def copy(src, dst, send, recv, to):
        return pltpu.make_async_remote_copy(
            src_ref=src, dst_ref=dst, send_sem=send, recv_sem=recv, device_id=to, device_id_type=MESH
        )

    barrier = pltpu.get_barrier_semaphore()
    for peer in (sib, up, down, right, left):
        pl.semaphore_signal(barrier, inc=1, device_id=peer, device_id_type=MESH)

    def greet(d, carry):
        pl.semaphore_signal(barrier, inc=1, device_id=at(y, z + d, core), device_id_type=MESH)
        return carry

    lax.fori_loop(1, nz, greet, 0)
    pl.semaphore_wait(barrier, 5 + nz - 1)

    sent = []

    def go(*args):
        c = copy(*args)
        c.start()
        sent.append(c)
        return c

    go(w_ref, wall.at[0], s_w.at[0], r_w.at[0], right)
    go(w_ref, wall.at[1], s_w.at[1], r_w.at[1], left)

    def landed(dst, recv):
        copy(dst, dst, recv, recv, sib).wait_recv()

    own = pl.multiple_of(core * half, half)
    other = pl.multiple_of((1 - core) * half, half)

    def stage_a(t):
        if t == 1:
            landed(wall.at[0], r_w.at[0])
            go(wall.at[0, :half], wall.at[2, :half], s_w.at[2], r_w.at[2], right)
            landed(wall.at[1], r_w.at[1])
            go(wall.at[1, half:], wall.at[2, half:], s_w.at[3], r_w.at[3], left)
        if t == 3:
            landed(wall.at[2, :half], r_w.at[2])
            landed(wall.at[2, half:], r_w.at[3])
        w = w_ref if t == 0 else wall.at[t - 1]
        w_both = jnp.concatenate([w[pl.ds(other, half), :], w[pl.ds(own, half), :]], axis=0)

        def block(b, carry):
            got = lax.dot_general(
                w_both, f_ref[pl.ds(pl.multiple_of(b * cols, cols), cols), :], NT,
                preferred_element_type=F32,
            )
            sibtx[t, b] = got[:half].astype(BF16)
            part[t, b] = got[half:]
            return carry

        lax.fori_loop(0, NY, block, 0)
        go(sibtx.at[t], sibrx.at[t], s_sib.at[t], r_sib.at[t], sib)

    def stage_b(t):
        landed(sibrx.at[t], r_sib.at[t])

        def block(b, carry):
            part[t, b] = part[t, b] + sibrx[t, b].astype(F32)
            return carry

        lax.fori_loop(0, NY, block, 0)
        ytx1[t] = part[t, lax.rem(y + 2, NY)].astype(BF16)
        go(ytx1.at[t, :mid], yrx1.at[t, 0], s_y1.at[t, 0], r_y1.at[t, 0], up)
        go(ytx1.at[t, mid:], yrx1.at[t, 1], s_y1.at[t, 1], r_y1.at[t, 1], down)

    def stage_c(t):
        above, below = lax.rem(y + 1, NY), lax.rem(y + NY - 1, NY)
        landed(yrx1.at[t, 0], r_y1.at[t, 0])
        ytx2[t, 0, :mid] = (part[t, above, :mid] + yrx1[t, 0].astype(F32)).astype(BF16)
        ytx2[t, 0, mid:] = part[t, above, mid:].astype(BF16)
        go(ytx2.at[t, 0], yrx2.at[t, 0], s_y2.at[t, 0], r_y2.at[t, 0], up)
        landed(yrx1.at[t, 1], r_y1.at[t, 1])
        ytx2[t, 1, :mid] = part[t, below, :mid].astype(BF16)
        ytx2[t, 1, mid:] = (part[t, below, mid:] + yrx1[t, 1].astype(F32)).astype(BF16)
        go(ytx2.at[t, 1], yrx2.at[t, 1], s_y2.at[t, 1], r_y2.at[t, 1], down)

    def z_copy(t, d):
        to = lax.rem(z + d, nz)
        return copy(ztx.at[t, to], zrx.at[t, d], s_z.at[t, d], r_z.at[t, d], at(y, z + d, core))

    def stage_d(t):
        landed(yrx2.at[t, 0], r_y2.at[t, 0])
        landed(yrx2.at[t, 1], r_y2.at[t, 1])
        total = part[t, y] + yrx2[t, 0].astype(F32) + yrx2[t, 1].astype(F32)
        ztx[t] = total.reshape(nz, seg, cols)

        def send(d, carry):
            z_copy(t, d).start()
            return carry

        lax.fori_loop(1, nz, send, 0)

    def g_copy(t, d):
        mine = xt.at[t, y, pl.ds(pl.multiple_of(core * half + z * seg, seg), seg), :]
        return copy(mine, mine, s_gz.at[t, d], r_gz.at[t, d], at(y, z + d, core))

    def stage_e(t):
        def add(d, total):
            landed(zrx.at[t, d], r_z.at[t, d])
            return total + zrx[t, d]

        total = lax.fori_loop(1, nz, add, ztx[t, z])
        xt[t, y, pl.ds(pl.multiple_of(core * half + z * seg, seg), seg), :] = total.astype(BF16)

        def send(d, carry):
            g_copy(t, d).start()
            return carry

        lax.fori_loop(1, nz, send, 0)

    def half_of(t, y_, start, size):
        first = pl.multiple_of(core * half + start, mid)
        return xt.at[t, lax.rem(y_ + NY, NY), pl.ds(first, size), :]

    def stage_f(t):
        def wait(d, carry):
            g_copy(t, d).wait_recv()
            return carry

        lax.fori_loop(1, nz, wait, 0)
        mine = half_of(t, y, 0, half)
        go(mine, mine, s_gy.at[t, 0], r_gy.at[t, 0], up)
        go(mine, mine, s_gy.at[t, 1], r_gy.at[t, 1], down)
        go(mine, mine, s_gs.at[t, 0], r_gs.at[t, 0], sib)

    def stage_g(t):
        landed(half_of(t, y - 1, 0, half), r_gy.at[t, 0])
        piece = half_of(t, y - 1, 0, mid)
        go(piece, piece, s_gy.at[t, 2], r_gy.at[t, 2], up)
        landed(half_of(t, y + 1, 0, half), r_gy.at[t, 1])
        piece = half_of(t, y + 1, mid, mid)
        go(piece, piece, s_gy.at[t, 3], r_gy.at[t, 3], down)
        for k, d in ((1, -1), (2, 1)):
            piece = half_of(t, y + d, 0, half)
            go(piece, piece, s_gs.at[t, k], r_gs.at[t, k], sib)

    def stage_h(t):
        landed(half_of(t, y + 2, 0, mid), r_gy.at[t, 2])
        landed(half_of(t, y + 2, mid, mid), r_gy.at[t, 3])
        piece = half_of(t, y + 2, 0, half)
        go(piece, piece, s_gs.at[t, 3], r_gs.at[t, 3], sib)

    def stage_i(t):
        for k in range(4):
            landed(half_of(t, y, 0, half), r_gs.at[t, k])

        def block(b, carry):
            got = jnp.dot(
                xt[t, b], f_ref[pl.ds(pl.multiple_of(b * cols, cols), cols), :],
                preferred_element_type=F32,
            )
            acc[min(t, 1)] = jnp.where(b == 0, got, acc[min(t, 1)] + got)
            return carry

        lax.fori_loop(0, NY, block, 0)
        if t:
            ptx[t - 1] = acc[1].astype(BF16)
        if t == 1:
            go(ptx.at[0], prx.at[1], s_p.at[1], r_p.at[1], left)
        if t == 2:
            go(ptx.at[1], prx.at[0], s_p.at[0], r_p.at[0], right)
        if t == 3:
            go(ptx.at[2, :half], relay.at[0], s_p.at[2], r_p.at[2], right)
            go(ptx.at[2, half:], relay.at[1], s_p.at[3], r_p.at[3], left)

    stages = (
        stage_a, stage_b, stage_c, stage_d, stage_e, stage_f, stage_g, stage_h, stage_i,
    )
    for step in range(len(stages) + nx - 1):
        for k in reversed(range(len(stages))):
            if 0 <= step - k < nx:
                stages[k](step - k)

    landed(relay.at[0], r_p.at[2])
    go(relay.at[0], prx.at[2, :half], s_p.at[4], r_p.at[4], right)
    landed(relay.at[1], r_p.at[3])
    go(relay.at[1], prx.at[2, half:], s_p.at[5], r_p.at[5], left)
    landed(prx.at[0], r_p.at[0])
    landed(prx.at[1], r_p.at[1])
    landed(prx.at[2, :half], r_p.at[4])
    landed(prx.at[2, half:], r_p.at[5])
    total = acc[0] + prx[0].astype(F32) + prx[1].astype(F32) + prx[2].astype(F32)
    out_ref[...] = total.astype(BF16)
    for c in sent:
        c.wait_send()
    for t in range(nx):
        def drain(d, carry, t=t):
            z_copy(t, d).wait_send()
            g_copy(t, d).wait_send()
            return carry

        lax.fori_loop(1, nz, drain, 0)


def middle(factors, weights):
    rows, width = weights.shape
    nx = lax.axis_size("aux")
    nz = lax.axis_size("pair") // (2 * NY)
    half, cols = rows // 2, factors.shape[0] // NY
    seg, mid = half // nz, half // 2
    dma = pltpu.SemaphoreType.DMA
    vmem = pl.BlockSpec(memory_space=pltpu.VMEM)
    pairs = [(4,), (nx,), (nx, 2), (nx, 2), (nx, nz), (nx, nz), (nx, 4), (nx, 4), (6,)]
    return pl.pallas_call(
        functools.partial(middle_kernel, nz, nx),
        out_shape=jax.ShapeDtypeStruct((rows, width), BF16),
        in_specs=[vmem, vmem],
        out_specs=vmem,
        scratch_shapes=[
            pltpu.VMEM((3, rows, width), BF16),
            pltpu.VMEM((nx, NY, half, cols), BF16),
            pltpu.VMEM((nx, NY, half, cols), BF16),
            pltpu.VMEM((nx, NY, half, cols), F32),
            pltpu.VMEM((nx, half, cols), BF16),
            pltpu.VMEM((nx, 2, mid, cols), BF16),
            pltpu.VMEM((nx, 2, half, cols), BF16),
            pltpu.VMEM((nx, 2, half, cols), BF16),
            pltpu.VMEM((nx, nz, seg, cols), F32),
            pltpu.VMEM((nx, nz, seg, cols), F32),
            pltpu.VMEM((nx, NY, rows, cols), BF16),
            pltpu.VMEM((3, rows, width), BF16),
            pltpu.VMEM((3, rows, width), BF16),
            pltpu.VMEM((2, half, width), BF16),
            pltpu.VMEM((2, rows, width), F32),
        ]
        + [dma(shape) for shape in pairs for _ in range(2)],
        compiler_params=pltpu.CompilerParams(
            collective_id=0, has_side_effects=True, vmem_limit_bytes=56 << 20
        ),
        cost_estimate=pl.CostEstimate(
            flops=4 * nx * rows * width * factors.shape[0], bytes_accessed=8 << 20, transcendentals=0
        ),
    )(factors, weights)


def on_device(factors, amplitudes, block_list, owner_map):
    pair_count = lax.axis_size("pair")
    aux_count = lax.axis_size("aux")
    me = lax.axis_index("pair")
    share = lax.axis_index("aux")
    block_count, block_width, _ = amplitudes.shape
    virt = factors.shape[2]
    part = block_width // aux_count
    slot_total = pair_count * CAP
    ids = lax.iota(jnp.int32, block_count)
    hits = block_list[:, 0][:, None] == lax.iota(jnp.int32, owner_map.shape[0])[None, :]
    owners = jnp.sum(jnp.where(hits, owner_map[None, :], 0), axis=1)
    codes = owners * (virt * virt) + block_list[:, 1] * virt + block_list[:, 2]
    same = (owners[:, None] == owners[None, :]) & (ids[None, :] < ids[:, None])
    slots = owners * CAP + jnp.sum(same.astype(jnp.int32), axis=1)
    placing = (slots[:, None] == lax.iota(jnp.int32, slot_total)[None, :]).astype(BF16)
    all_codes = lax.all_gather(codes, "pair", axis=0, tiled=False)
    mine = lax.dynamic_slice_in_dim(amplitudes, share * part, part, axis=1)
    sent = jnp.einsum("js,jm->sm", placing, mine.reshape(block_count, -1), preferred_element_type=F32)
    sent = sent.astype(BF16).reshape(pair_count, CAP, part, block_width)
    got = lax.all_to_all(sent, "pair", split_axis=0, concat_axis=0, tiled=True)
    ours = all_codes // (virt * virt) == me
    combos = all_codes % (virt * virt)
    first = jnp.min(jnp.where(ours, ids[None, :], block_count), axis=1)
    last = jnp.max(jnp.where(ours, ids[None, :], -1), axis=1)
    at_first = ours & (ids[None, :] == first[:, None])
    at_second = ours & (ids[None, :] == last[:, None]) & (last > first)[:, None]
    combo0 = jnp.sum(jnp.where(at_first, combos + 1, 0), axis=1) - 1
    combo1 = jnp.sum(jnp.where(at_second, combos + 1, 0), axis=1) - 1
    slot_combo = jnp.stack([combo0, combo1], axis=1).reshape(slot_total)
    picks = (slot_combo[:, None] == lax.iota(jnp.int32, virt * virt)[None, :]).astype(BF16)
    weights = jnp.einsum(
        "sn,sm->nm", picks, got.reshape(slot_total, -1), preferred_element_type=F32
    ).astype(BF16)
    weights = weights.reshape(virt, virt, part, block_width).transpose(0, 2, 1, 3)
    out = middle(
        factors.reshape(-1, virt * block_width), weights.reshape(virt * part, virt * block_width)
    )
    out = out.astype(BF16).reshape(virt, part, virt, block_width).transpose(0, 2, 1, 3)
    back = jnp.einsum(
        "sn,nm->sm", picks, out.reshape(virt * virt, -1), preferred_element_type=F32
    )
    back = back.astype(BF16).reshape(pair_count, CAP, part, block_width)
    back = lax.all_to_all(back, "pair", split_axis=0, concat_axis=0, tiled=True)
    result = jnp.einsum(
        "js,sm->jm", placing, back.reshape(slot_total, -1), preferred_element_type=F32
    )
    result = result.astype(BF16).reshape(block_count, part, block_width)
    return lax.all_gather(result, "aux", axis=1, tiled=True)


def solution(mesh):
    placed = (P("pair", "aux", None, None), P("pair", None, None), P("pair", None), P())
    return jax.shard_map(
        on_device, mesh=mesh, in_specs=placed, out_specs=P("pair", None, None), check_vma=False
    )
```

time: 619 us -> 270 us (0.44)
  waiting for transfers between devices: 326 us -> 25.1 us
  Pallas kernels: 0 us -> 102 us
  blocking collectives: 182 us -> 99.8 us
  local copies, waits for them, and re-layouts: 42.2 us -> 13.3 us
  matrix products: 29.8 us -> 2.01 us
  starting transfers between devices: 21 us -> 13.2 us
    reduce_scatter x1 -> x0, waiting for transfers between devices: 144 us -> none  [on_device(): lax.psum_scatter(jnp.dot(factor_rows, weights, preferred_element_type=jnp...]
    pallas_call x0 -> x1, Pallas kernels: none -> 102 us  [middle(): pl.pallas_call(functools.partial(middle_kernel, nz, nx), out_shape=jax.Sh...]
    all_to_all x2 -> x1, waiting for transfers between devices: 98.4 us -> 0.01 us  [on_device(): got = lax.all_to_all(sent, 'pair', split_axis=0, concat_axis=0, tiled=True)]
    psum x1 -> x0, blocking collectives: 78.1 us -> none  [on_device(): summed = lax.psum(projected, 'aux')]
    all_to_all x1, blocking collectives: 104 us -> 40.5 us  [on_device(): back = lax.all_to_all(back, 'pair', split_axis=0, concat_axis=0, tiled=True)]
    all_gather x0 -> x1, blocking collectives: none -> 59.3 us  [on_device(): all_codes = lax.all_gather(codes, 'pair', axis=0, tiled=False)]
    all_gather x1, waiting for transfers between devices: 83.6 us -> 25.1 us  [on_device(): return lax.all_gather(result, 'aux', axis=1, tiled=True)]
    dot_general x5 -> x4, matrix products: 29.8 us -> 2.01 us  [the longest x1 0.55 us: on_device(): jnp.einsum('js,jm->sm', placing, mine.reshape(block_count, -1), preferred...]
  transfers between devices with their start and end apart: 4 -> 2, of which waited for: 4 -> 1; matrix products, arithmetic and copies ran while one was open for 1% -> 2% of each run, Pallas kernels for 0% -> 0%
where the time goes in v1:
time: 270 us
  Pallas kernels  102 us (38%)
  blocking collectives  99.8 us (37%)
  waiting for transfers between devices  25.1 us (9%)
  between operations  13.5 us (5%)
  local copies, waits for them, and re-layouts  13.3 us (5%)
  starting transfers between devices  13.2 us (5%)
    pallas_call x1, Pallas kernels, middle(): pl.pallas_call(functools.partial(middle_kernel, nz, nx), out_shape=jax.Sh...  102 us
    all_gather x1, blocking collectives, on_device(): all_codes = lax.all_gather(codes, 'pair', axis=0, tiled=False)  59.3 us
    all_to_all x1, blocking collectives, on_device(): back = lax.all_to_all(back, 'pair', split_axis=0, concat_axis=0, tiled=True)  40.5 us
    all_gather x1, waiting for transfers between devices, on_device(): return lax.all_gather(result, 'aux', axis=1, tiled=True)  25.1 us
    all_to_all x1, starting transfers between devices, on_device(): got = lax.all_to_all(sent, 'pair', split_axis=0, concat_axis=0, tiled=True)  13.2 us
    unnamed x11, local copies, waits for them, and re-layouts  12.2 us
  transfers between devices with their start and end apart: 2, of which 1 were waited for; matrix products, arithmetic and copies ran while one was open for 2% of the time, Pallas kernels for 0%

profile of v1, /device:TPU:1, one launch (start us, length us, event | category | flops | bytes accessed | tf_op | source)
XLA Modules:
  0.0 269.9 jit_solution(5557750365467405243)
XLA Ops:
  6.5 0.0 copy-start
  6.5 0.8 slice_bitcast_fusion
  7.3 0.8 select_reduce_fusion.4
  8.2 0.2 convert_reduce_fusion
  8.4 0.0 copy-done
  8.4 0.5 fusion.1
  9.0 0.0 copy-start.1
  9.0 1.2 copy.11
  10.2 13.2 %all-to-all-start = ((bf16[64,2,32,128]{3,2,1,0:T(8,128)(2,1)}), bf16[64,2,32,128]{3,2,1,0:T(8,128)(2,1)S(1)}, u32[]{:S(2)}, u32[]{:S(2)}) async-start(bf16[64,2,32,128]{3,2,1,0:T(8,128)(2,1)} %bitcast.72), calls=%async_computation | async-start | bytes 2097152 | tf_op jit(solution)/shard_map/all_to_all | solution.py:297
  23.3 0.0 all-gather.3.cloned.1.call-start
  23.4 0.0 copy-done.1
  23.4 59.3 %all-gather = s32[64,1,48]{2,1,0:T(1,128)S(1)} all-gather(s32[1,1,48]{2,1,0:T(1,128)S(1)} %fusion.21), channel_id=1, replica_groups=mesh['pair'=64,'aux'=4] {'pair'}, dimensions={0}, use_global_device_ids=true | all-gather | bytes 12480 | tf_op jit(solution)/shard_map/all_gather | solution.py:293
  82.8 0.1 select_reduce_fusion.3
  82.9 0.2 select_reduce_fusion.2
  83.1 0.1 copy.8
  83.2 0.1 eq.114
  83.4 5.2 %copy.32 = bf16[256,8,8,128]{3,1,2,0:T(8,128)(2,1)} copy(bf16[256,8,8,128]{3,2,1,0:T(8,128)(2,1)} %bitcast.69) | data formatting | bytes 8388608
  88.6 0.0 all-to-all-done
  88.6 0.5 convolution_convert_fusion.2
  89.1 0.9 copy.33
  90.0 101.5 %shard_map.46 = bf16[256,1024]{1,0:T(8,128)(2,1)} custom-call(bf16[2048,1024]{1,0:T(8,128)(2,1)} %bitcast.70, bf16[256,1024]{1,0:T(8,128)(2,1)} %bitcast.79), custom_call_target="tpu_custom_call" | custom-call | flops 8589934592 | bytes 8388608 | tf_op jit(solution)/shard_map/pallas_call | solution.py:245
  191.5 1.1 copy.14
  192.7 0.5 fusion
  193.2 0.2 copy.15
  193.4 40.5 %all_to_all.10 = bf16[64,2,32,128]{3,2,1,0:T(8,128)(2,1)S(1)} all-to-all(bf16[64,2,32,128]{3,2,1,0:T(8,128)(2,1)S(1)} %bitcast.74), channel_id=1, replica_groups=mesh['pair'=64,'aux'=4] {'pair'}, dimensions={0} | all-to-all | bytes 2097152 | tf_op jit(solution)/shard_map/all_to_all | solution.py:320
  233.9 0.5 fusion.2
  234.4 0.8 copy.17
  235.2 0.0 all-gather.3.cloned.1.call-update
  235.2 25.1 %all-gather.3.cloned.1.call-done = bf16[48,128,128]{2,1,0:T(8,128)(2,1)} async-done(((bf16[48,32,128]{2,1,0:T(8,128)(2,1)}), bf16[48,128,128]{2,1,0:T(8,128)(2,1)}) %all-gather.3.cloned.1.call-update) | async-done | bytes 1572880 | tf_op jit(solution)/shard_map/all_gather | solution.py:325
  260.3 2.7 %copy.35 = bf16[48,128,128]{2,1,0:T(8,128)(2,1)} copy(bf16[48,128,128]{2,1,0:T(8,128)(2,1)} %all-gather.3.cloned.1.call-done) | data formatting | bytes 3145728
  (6 shorter events, 0.1 us)
Async XLA Ops:
  6.5 1.8 copy-start
  9.0 14.4 %copy-start.1 = (s32[48,3]{0,1:T(4,128)S(1)}, s32[48,3]{0,1:T(4,128)}, u32[]{:S(2)}) copy-start(s32[48,3]{0,1:T(4,128)} %param.6) | copy-start | bytes 1732
  10.2 78.4 %all-to-all-start = ((bf16[64,2,32,128]{3,2,1,0:T(8,128)(2,1)}), bf16[64,2,32,128]{3,2,1,0:T(8,128)(2,1)S(1)}, u32[]{:S(2)}, u32[]{:S(2)}) async-start(bf16[64,2,32,128]{3,2,1,0:T(8,128)(2,1)} %bitcast.72), calls=%async_computation | async-start | bytes 2097152 | tf_op jit(solution)/shard_map/all_to_all | solution.py:297
  23.3 236.9 %all-gather.3.cloned.1.call-start = ((), (), s32[]{:S(2)}) async-start(), calls=%async_computation.2 | async-start | bytes 1966080 | tf_op jit(solution)/shard_map/all_gather | solution.py:325
Sparse Core Ops, SparseCore 0:
  235.3 24.9 all-gather.2

commit v2 on v1

--- a/solution.py
+++ b/solution.py
@@ -68,7 +68,7 @@
     own = pl.multiple_of(core * half, half)
     other = pl.multiple_of((1 - core) * half, half)
 
-    def stage_a(t):
+    def weights_product(t):
         if t == 1:
             landed(wall.at[0], r_w.at[0])
             go(wall.at[0, :half], wall.at[2, :half], s_w.at[2], r_w.at[2], right)
@@ -92,7 +92,7 @@
         lax.fori_loop(0, NY, block, 0)
         go(sibtx.at[t], sibrx.at[t], s_sib.at[t], r_sib.at[t], sib)
 
-    def stage_b(t):
+    def core_sum(t):
         landed(sibrx.at[t], r_sib.at[t])
 
         def block(b, carry):
@@ -104,7 +104,7 @@
         go(ytx1.at[t, :mid], yrx1.at[t, 0], s_y1.at[t, 0], r_y1.at[t, 0], up)
         go(ytx1.at[t, mid:], yrx1.at[t, 1], s_y1.at[t, 1], r_y1.at[t, 1], down)
 
-    def stage_c(t):
+    def y_relay_sum(t):
         above, below = lax.rem(y + 1, NY), lax.rem(y + NY - 1, NY)
         landed(yrx1.at[t, 0], r_y1.at[t, 0])
         ytx2[t, 0, :mid] = (part[t, above, :mid] + yrx1[t, 0].astype(F32)).astype(BF16)
@@ -119,7 +119,7 @@
         to = lax.rem(z + d, nz)
         return copy(ztx.at[t, to], zrx.at[t, d], s_z.at[t, d], r_z.at[t, d], at(y, z + d, core))
 
-    def stage_d(t):
+    def y_sum(t):
         landed(yrx2.at[t, 0], r_y2.at[t, 0])
         landed(yrx2.at[t, 1], r_y2.at[t, 1])
         total = part[t, y] + yrx2[t, 0].astype(F32) + yrx2[t, 1].astype(F32)
@@ -135,7 +135,7 @@
         mine = xt.at[t, y, pl.ds(pl.multiple_of(core * half + z * seg, seg), seg), :]
         return copy(mine, mine, s_gz.at[t, d], r_gz.at[t, d], at(y, z + d, core))
 
-    def stage_e(t):
+    def z_sum(t):
         def add(d, total):
             landed(zrx.at[t, d], r_z.at[t, d])
             return total + zrx[t, d]
@@ -153,7 +153,7 @@
         first = pl.multiple_of(core * half + start, mid)
         return xt.at[t, lax.rem(y_ + NY, NY), pl.ds(first, size), :]
 
-    def stage_f(t):
+    def z_gather(t):
         def wait(d, carry):
             g_copy(t, d).wait_recv()
             return carry
@@ -164,7 +164,7 @@
         go(mine, mine, s_gy.at[t, 1], r_gy.at[t, 1], down)
         go(mine, mine, s_gs.at[t, 0], r_gs.at[t, 0], sib)
 
-    def stage_g(t):
+    def y_gather(t):
         landed(half_of(t, y - 1, 0, half), r_gy.at[t, 0])
         piece = half_of(t, y - 1, 0, mid)
         go(piece, piece, s_gy.at[t, 2], r_gy.at[t, 2], up)
@@ -175,13 +175,13 @@
             piece = half_of(t, y + d, 0, half)
             go(piece, piece, s_gs.at[t, k], r_gs.at[t, k], sib)
 
-    def stage_h(t):
+    def y_relay_gather(t):
         landed(half_of(t, y + 2, 0, mid), r_gy.at[t, 2])
         landed(half_of(t, y + 2, mid, mid), r_gy.at[t, 3])
         piece = half_of(t, y + 2, 0, half)
         go(piece, piece, s_gs.at[t, 3], r_gs.at[t, 3], sib)
 
-    def stage_i(t):
+    def block_product(t):
         for k in range(4):
             landed(half_of(t, y, 0, half), r_gs.at[t, k])
 
@@ -205,12 +205,13 @@
             go(ptx.at[2, half:], relay.at[1], s_p.at[3], r_p.at[3], left)
 
     stages = (
-        stage_a, stage_b, stage_c, stage_d, stage_e, stage_f, stage_g, stage_h, stage_i,
+        weights_product, core_sum, y_relay_sum, y_sum, z_sum, z_gather, y_gather, y_relay_gather, block_product,
     )
     for step in range(len(stages) + nx - 1):
         for k in reversed(range(len(stages))):
             if 0 <= step - k < nx:
-                stages[k](step - k)
+                with jax.named_scope(f"{stages[k].__name__}_chunk{step - k}"):
+                    stages[k](step - k)
 
     landed(relay.at[0], r_p.at[2])
     go(relay.at[0], prx.at[2, :half], s_p.at[4], r_p.at[4], right)
@@ -273,56 +274,224 @@
         ),
     )(factors, weights)
 
+def exchange_kernel(n, send_ref, meta_ref, f_ref, got_ref, gmeta_ref, flat_ref, s_d, r_d, s_m, r_m):
+    me = lax.axis_index("pair")
+    barrier = pltpu.get_barrier_semaphore()
+
+    def greet(d, carry):
+        pl.semaphore_signal(
+            barrier, inc=1, device_id={"pair": lax.rem(me + d, n)}, device_id_type=MESH
+        )
+        return carry
+
+    lax.fori_loop(1, n, greet, 0)
+    pl.semaphore_wait(barrier, n - 1)
+
+    def copies(d):
+        to = lax.rem(me + d, n)
+        return (
+            pltpu.make_async_remote_copy(
+                src_ref=meta_ref.at[to], dst_ref=gmeta_ref.at[me], send_sem=s_m.at[d],
+                recv_sem=r_m.at[d], device_id={"pair": to}, device_id_type=MESH,
+            ),
+            pltpu.make_async_remote_copy(
+                src_ref=send_ref.at[to], dst_ref=got_ref.at[me], send_sem=s_d.at[d],
+                recv_sem=r_d.at[d], device_id={"pair": to}, device_id_type=MESH,
+            ),
+        )
+
+    def start(d, carry):
+        for c in copies(d):
+            c.start()
+        return carry
+
+    lax.fori_loop(1, n, start, 0)
+    got_ref[me] = send_ref[me]
+    gmeta_ref[me] = meta_ref[me]
+    step = 64 if f_ref.shape[0] % 64 == 0 else f_ref.shape[0]
+
+    def flatten(i, carry):
+        rows = pl.ds(pl.multiple_of(i * step, step), step)
+        flat_ref[rows, :] = f_ref[rows].astype(F32).reshape(step, -1).astype(BF16)
+        return carry
+
+    lax.fori_loop(0, f_ref.shape[0] // step, flatten, 0)
+
+    def finish(d, carry):
+        for c in copies(d):
+            c.wait()
+        return carry
+
+    lax.fori_loop(1, n, finish, 0)
+
+
+def exchange(send, meta, factors):
+    n = send.shape[0]
+    dma = pltpu.SemaphoreType.DMA
+    vmem = pl.BlockSpec(memory_space=pltpu.VMEM)
+    return pl.pallas_call(
+        functools.partial(exchange_kernel, n),
+        out_shape=(
+            jax.ShapeDtypeStruct(send.shape, send.dtype),
+            jax.ShapeDtypeStruct(meta.shape, meta.dtype),
+            jax.ShapeDtypeStruct((factors.shape[0], factors.shape[1] * factors.shape[2]), BF16),
+        ),
+        in_specs=[vmem] * 3,
+        out_specs=(vmem,) * 3,
+        scratch_shapes=[dma((n,))] * 4,
+        compiler_params=pltpu.CompilerParams(
+            collective_id=1, has_side_effects=True, vmem_limit_bytes=40 << 20
+        ),
+    )(send, meta, factors)
+
+
+def back_kernel(n, send_ref, got_ref, s_d, r_d):
+    me = lax.axis_index("pair")
+    barrier = pltpu.get_barrier_semaphore()
+
+    def greet(d, carry):
+        pl.semaphore_signal(
+            barrier, inc=1, device_id={"pair": lax.rem(me + d, n)}, device_id_type=MESH
+        )
+        return carry
+
+    lax.fori_loop(1, n, greet, 0)
+    pl.semaphore_wait(barrier, n - 1)
+
+    def message(d):
+        to = lax.rem(me + d, n)
+        return pltpu.make_async_remote_copy(
+            src_ref=send_ref.at[to], dst_ref=got_ref.at[me], send_sem=s_d.at[d],
+            recv_sem=r_d.at[d], device_id={"pair": to}, device_id_type=MESH,
+        )
+
+    def start(d, carry):
+        message(d).start()
+        return carry
+
+    lax.fori_loop(1, n, start, 0)
+    got_ref[me] = send_ref[me]
+
+    def finish(d, carry):
+        message(d).wait()
+        return carry
+
+    lax.fori_loop(1, n, finish, 0)
+
+
+def send_back(send):
+    n = send.shape[0]
+    dma = pltpu.SemaphoreType.DMA
+    vmem = pl.BlockSpec(memory_space=pltpu.VMEM)
+    return pl.pallas_call(
+        functools.partial(back_kernel, n),
+        out_shape=jax.ShapeDtypeStruct(send.shape, send.dtype),
+        in_specs=[vmem],
+        out_specs=vmem,
+        scratch_shapes=[dma((n,))] * 2,
+        compiler_params=pltpu.CompilerParams(
+            collective_id=2, has_side_effects=True, vmem_limit_bytes=24 << 20
+        ),
+    )(send)
+
+
+def join_kernel(nx, part_ref, out_ref, s_d, r_d):
+    aux = lax.axis_index("aux")
+    right, left = {"aux": lax.rem(aux + 1, nx)}, {"aux": lax.rem(aux + nx - 1, nx)}
+    barrier = pltpu.get_barrier_semaphore()
+    for peer in (right, left):
+        pl.semaphore_signal(barrier, inc=1, device_id=peer, device_id_type=MESH)
+    pl.semaphore_wait(barrier, 2)
+    count, part, _ = part_ref.shape
+    half = count // 2
+
+    def place(who, first, size):
+        rows = pl.ds(pl.multiple_of(lax.rem(who + nx, nx) * part, part), part)
+        return out_ref.at[pl.ds(first, size), rows, :]
+
+    def copy(src, dst, k, to):
+        return pltpu.make_async_remote_copy(
+            src_ref=src, dst_ref=dst, send_sem=s_d.at[k], recv_sem=r_d.at[k], device_id=to,
+            device_id_type=MESH,
+        )
+
+    own = [
+        copy(part_ref.at[:half], place(aux, 0, half), 0, right),
+        copy(part_ref.at[half:], place(aux, half, half), 1, left),
+        copy(part_ref.at[half:], place(aux, half, half), 2, right),
+        copy(part_ref.at[:half], place(aux, 0, half), 3, left),
+    ]
+    for c in own:
+        c.start()
+    out_ref[:, pl.ds(pl.multiple_of(aux * part, part), part), :] = part_ref[...]
+    low, high = place(aux - 1, 0, half), place(aux + 1, half, half)
+    on = [copy(low, low, 4, right), copy(high, high, 5, left)]
+    own[0].wait_recv()
+    on[0].start()
+    own[1].wait_recv()
+    on[1].start()
+    for c in own[2:] + on:
+        c.wait_recv()
+    for c in own + on:
+        c.wait_send()
+
+
+def join(part):
+    nx = lax.axis_size("aux")
+    count, rows, width = part.shape
+    dma = pltpu.SemaphoreType.DMA
+    vmem = pl.BlockSpec(memory_space=pltpu.VMEM)
+    return pl.pallas_call(
+        functools.partial(join_kernel, nx),
+        out_shape=jax.ShapeDtypeStruct((count, nx * rows, width), part.dtype),
+        in_specs=[vmem],
+        out_specs=vmem,
+        scratch_shapes=[dma((6,))] * 2,
+        compiler_params=pltpu.CompilerParams(
+            collective_id=3, has_side_effects=True, vmem_limit_bytes=24 << 20
+        ),
+    )(part)
+
 
 def on_device(factors, amplitudes, block_list, owner_map):
     pair_count = lax.axis_size("pair")
     aux_count = lax.axis_size("aux")
-    me = lax.axis_index("pair")
     share = lax.axis_index("aux")
     block_count, block_width, _ = amplitudes.shape
     virt = factors.shape[2]
+    combos = virt * virt
     part = block_width // aux_count
     slot_total = pair_count * CAP
     ids = lax.iota(jnp.int32, block_count)
     hits = block_list[:, 0][:, None] == lax.iota(jnp.int32, owner_map.shape[0])[None, :]
     owners = jnp.sum(jnp.where(hits, owner_map[None, :], 0), axis=1)
-    codes = owners * (virt * virt) + block_list[:, 1] * virt + block_list[:, 2]
+    combo = block_list[:, 1] * virt + block_list[:, 2]
     same = (owners[:, None] == owners[None, :]) & (ids[None, :] < ids[:, None])
     slots = owners * CAP + jnp.sum(same.astype(jnp.int32), axis=1)
     placing = (slots[:, None] == lax.iota(jnp.int32, slot_total)[None, :]).astype(BF16)
-    all_codes = lax.all_gather(codes, "pair", axis=0, tiled=False)
+    at_combo = (combo[:, None] == lax.iota(jnp.int32, combos)[None, :]).astype(BF16)
+    picks_out = jnp.einsum("js,jn->sn", placing, at_combo, preferred_element_type=F32)
     mine = lax.dynamic_slice_in_dim(amplitudes, share * part, part, axis=1)
     sent = jnp.einsum("js,jm->sm", placing, mine.reshape(block_count, -1), preferred_element_type=F32)
     sent = sent.astype(BF16).reshape(pair_count, CAP, part, block_width)
-    got = lax.all_to_all(sent, "pair", split_axis=0, concat_axis=0, tiled=True)
-    ours = all_codes // (virt * virt) == me
-    combos = all_codes % (virt * virt)
-    first = jnp.min(jnp.where(ours, ids[None, :], block_count), axis=1)
-    last = jnp.max(jnp.where(ours, ids[None, :], -1), axis=1)
-    at_first = ours & (ids[None, :] == first[:, None])
-    at_second = ours & (ids[None, :] == last[:, None]) & (last > first)[:, None]
-    combo0 = jnp.sum(jnp.where(at_first, combos + 1, 0), axis=1) - 1
-    combo1 = jnp.sum(jnp.where(at_second, combos + 1, 0), axis=1) - 1
-    slot_combo = jnp.stack([combo0, combo1], axis=1).reshape(slot_total)
-    picks = (slot_combo[:, None] == lax.iota(jnp.int32, virt * virt)[None, :]).astype(BF16)
+    got, picks, flat = exchange(
+        sent, picks_out.reshape(pair_count, 1, CAP * combos), factors.reshape(-1, virt, block_width)
+    )
+    picks = picks.reshape(slot_total, combos).astype(BF16)
     weights = jnp.einsum(
         "sn,sm->nm", picks, got.reshape(slot_total, -1), preferred_element_type=F32
     ).astype(BF16)
     weights = weights.reshape(virt, virt, part, block_width).transpose(0, 2, 1, 3)
-    out = middle(
-        factors.reshape(-1, virt * block_width), weights.reshape(virt * part, virt * block_width)
+    out = middle(flat, weights.reshape(virt * part, virt * block_width))
+    out = out.reshape(virt, part, virt, block_width).transpose(0, 2, 1, 3)
+    back = jnp.einsum(
+        "sn,nm->sm", picks, out.reshape(combos, -1), preferred_element_type=F32
     )
-    out = out.astype(BF16).reshape(virt, part, virt, block_width).transpose(0, 2, 1, 3)
-    back = jnp.einsum(
-        "sn,nm->sm", picks, out.reshape(virt * virt, -1), preferred_element_type=F32
-    )
-    back = back.astype(BF16).reshape(pair_count, CAP, part, block_width)
-    back = lax.all_to_all(back, "pair", split_axis=0, concat_axis=0, tiled=True)
+    back = send_back(back.astype(BF16).reshape(pair_count, CAP, part, block_width))
     result = jnp.einsum(
         "js,sm->jm", placing, back.reshape(slot_total, -1), preferred_element_type=F32
     )
-    result = result.astype(BF16).reshape(block_count, part, block_width)
-    return lax.all_gather(result, "aux", axis=1, tiled=True)
+    return join(result.astype(BF16).reshape(block_count, part, block_width))
 
 
 def solution(mesh):

time: 270 us -> 209 us (0.77)
  blocking collectives: 99.8 us -> 0 us
  Pallas kernels: 102 us -> 198 us
  waiting for transfers between devices: 25.1 us -> 0 us
  between operations: 13.5 us -> 0.12 us
  starting transfers between devices: 13.2 us -> 0 us
  local copies, waits for them, and re-layouts: 13.3 us -> 7.19 us
    pallas_call x0 -> x3, Pallas kernels: none -> 88.5 us  [the longest x1 38.3 us: exchange(): pl.pallas_call(functools.partial(exchange_kernel, n), out_shape=(jax.Shap...]
    all_gather x1 -> x0, blocking collectives: 59.3 us -> none  [on_device(): all_codes = lax.all_gather(codes, 'pair', axis=0, tiled=False)]
    all_to_all x1 -> x0, blocking collectives: 40.5 us -> none  [on_device(): back = lax.all_to_all(back, 'pair', split_axis=0, concat_axis=0, tiled=True)]
    all_gather x1 -> x0, waiting for transfers between devices: 25.1 us -> none  [on_device(): return lax.all_gather(result, 'aux', axis=1, tiled=True)]
    all_to_all x1 -> x0, starting transfers between devices: 13.2 us -> none  [on_device(): got = lax.all_to_all(sent, 'pair', split_axis=0, concat_axis=0, tiled=True)]
    pallas_call x1, Pallas kernels: 102 us -> 109 us  [middle(): pl.pallas_call(functools.partial(middle_kernel, nz, nx), out_shape=jax.Sh...]
    unnamed x11 -> x12, local copies, waits for them, and re-layouts: 12.2 us -> 7 us
  transfers between devices with their start and end apart: 2 -> 0, of which waited for: 1 -> 0; matrix products, arithmetic and copies ran while one was open for 2% -> 0% of each run, Pallas kernels for 0% -> 0%
where the time goes in v2:
time: 209 us
  Pallas kernels  198 us (95%)
  local copies, waits for them, and re-layouts  7.19 us (3%)
  matrix products  2.22 us (1%)
    pallas_call x1, Pallas kernels, middle(): pl.pallas_call(functools.partial(middle_kernel, nz, nx), out_shape=jax.Sh...  109 us
    pallas_call x1, Pallas kernels, exchange(): pl.pallas_call(functools.partial(exchange_kernel, n), out_shape=(jax.Shap...  38.3 us
    pallas_call x1, Pallas kernels, send_back(): pl.pallas_call(functools.partial(back_kernel, n), out_shape=jax.ShapeDtyp...  32.8 us
    pallas_call x1, Pallas kernels, join(): pl.pallas_call(functools.partial(join_kernel, nx), out_shape=jax.ShapeDty...  17.4 us
    unnamed x12, local copies, waits for them, and re-layouts  7 us

profile of v2, /device:TPU:1, one launch (start us, length us, event | category | flops | bytes accessed | tf_op | source)
XLA Modules:
  0.0 209.3 jit_solution(16208965358639705541)
XLA Ops:
  0.0 0.0 copy-start
  0.0 0.8 add_bitcast_fusion
  0.8 0.8 select_reduce_fusion
  1.7 0.2 convert_reduce_fusion.1
  1.9 0.3 fusion.9
  2.2 0.1 reshape.50
  2.2 0.0 copy-done
  2.2 0.0 copy-start.1
  2.3 0.5 fusion.1
  2.8 0.2 copy.12
  3.1 1.4 copy-done.1
  4.4 38.3 %shard_map.46 = (bf16[64,2,32,128]{3,2,1,0:T(8,128)(2,1)S(1)}, f32[64,1,128]{2,1,0:T(1,128)S(1)}, bf16[2048,1024]{1,0:T(8,128)(2,1)S(1)}) custom-call(bf16[64,2,32,128]{3,2,1,0:T(8,128)(2,1)S(1)} %bitcast.54, f32[64,1,128]{2,1,0:T(1,128)S(1)} %bitcast.59, bf16[2048,8,128]{2,1,0:T(8,128)(2,1)S(1)} %bitcast.53), custom_call_target="tpu_custom_call" | custom-call | tf_op jit(solution)/shard_map/pallas_call | solution.py:332
  42.8 0.0 copy-start.2
  42.8 1.9 copy-done.2
  44.7 0.1 convert_reduce_fusion
  44.8 0.1 convert_element_type.27
  44.9 0.5 convolution_convert_fusion.2
  45.4 0.9 copy.32
  46.3 109.3 %shard_map.47 = bf16[256,1024]{1,0:T(8,128)(2,1)} custom-call(bf16[2048,1024]{1,0:T(8,128)(2,1)} %copy-done.2, bf16[256,1024]{1,0:T(8,128)(2,1)} %bitcast.63), custom_call_target="tpu_custom_call" | custom-call | flops 8589934592 | bytes 8388608 | tf_op jit(solution)/shard_map/pallas_call | solution.py:246
  155.6 1.1 copy.15
  156.7 0.4 fusion
  157.1 0.2 copy.16
  157.4 32.8 %shard_map.48 = bf16[64,2,32,128]{3,2,1,0:T(8,128)(2,1)S(1)} custom-call(bf16[64,2,32,128]{3,2,1,0:T(8,128)(2,1)S(1)} %bitcast.56), custom_call_target="tpu_custom_call" | custom-call | tf_op jit(solution)/shard_map/pallas_call | solution.py:386
  190.2 0.5 fusion.2
  190.6 0.1 copy.18
  190.7 17.4 %shard_map.49 = bf16[48,128,128]{2,1,0:T(8,128)(2,1)S(1)} custom-call(bf16[48,32,128]{2,1,0:T(8,128)(2,1)S(1)} %bitcast.57), custom_call_target="tpu_custom_call" | custom-call | tf_op jit(solution)/shard_map/pallas_call | solution.py:444
  208.1 1.1 copy.34
  (2 shorter events, 0.0 us)
Async XLA Ops:
  0.0 2.2 %copy-start = (bf16[48,128,128]{2,1,0:T(8,128)(2,1)S(1)}, bf16[48,128,128]{2,1,0:T(8,128)(2,1)}, u32[]{:S(2)}) copy-start(bf16[48,128,128]{2,1,0:T(8,128)(2,1)} %param.5) | copy-start | bytes 4718596
  2.2 2.2 %copy-start.1 = (bf16[1,2048,8,128]{3,2,1,0:T(8,128)(2,1)S(1)}, bf16[1,2048,8,128]{3,2,1,0:T(8,128)(2,1)}, u32[]{:S(2)}) copy-start(bf16[1,2048,8,128]{3,2,1,0:T(8,128)(2,1)} %param.4) | copy-start | bytes 12582916
  42.8 1.9 copy-start.2

commit v3 on v1

v3 whole, which is shorter than its diff:
```python
import functools

import jax
import jax.numpy as jnp
from jax import lax
from jax.experimental import pallas as pl
from jax.experimental.pallas import tpu as pltpu
from jax.sharding import PartitionSpec as P

CAP = 2
NY = 4
F32 = jnp.float32
BF16 = jnp.bfloat16
MESH = pl.DeviceIdType.MESH
NT = (((1,), (1,)), ((), ()))
TN = (((0,), (0,)), ((), ()))


def cycle_kernel(
    nz, nx, factor_ref, send_ref, meta_ref, place_ref, out_ref, f_ref, got_ref, picks_ref, bsend,
    bgot, w_ref, wall, sibtx, sibrx, part, ytx1, yrx1, ytx2, yrx2, ztx, zrx, xt, ptx, prx, relay,
    acc, s_m, r_m, s_a, r_a, s_b, r_b, s_j, r_j, s_w, r_w, s_sib, r_sib, s_y1, r_y1, s_y2, r_y2,
    s_z, r_z, s_gz, r_gz, s_gy, r_gy, s_gs, r_gs, s_p, r_p,
):
    pair, aux = lax.axis_index("pair"), lax.axis_index("aux")
    core, z, y = lax.rem(pair, 2), lax.rem(pair // 2, nz), pair // (2 * nz)
    half = sibtx.shape[2]
    seg = half // nz
    mid = half // 2
    cols = part.shape[3]
    rows = 2 * half

    def at(y_, z_, c_):
        return {"pair": (lax.rem(y_ + NY, NY) * nz + lax.rem(z_ + nz, nz)) * 2 + c_}

    sib = at(y, z, 1 - core)
    up, down = at(y + 1, z, core), at(y - 1, z, core)
    right, left = {"aux": lax.rem(aux + 1, nx)}, {"aux": lax.rem(aux + nx - 1, nx)}

    def copy(src, dst, send, recv, to):
        return pltpu.make_async_remote_copy(
            src_ref=src, dst_ref=dst, send_sem=send, recv_sem=recv, device_id=to, device_id_type=MESH
        )

    n = 2 * NY * nz
    barrier = pltpu.get_barrier_semaphore()
    for peer in (right, left):
        pl.semaphore_signal(barrier, inc=1, device_id=peer, device_id_type=MESH)

    def peer_at(d):
        return lax.rem(pair + d, n)

    def greet(d, carry):
        pl.semaphore_signal(
            barrier, inc=1, device_id={"pair": peer_at(d)}, device_id_type=MESH
        )
        return carry

    lax.fori_loop(1, n, greet, 0)
    pl.semaphore_wait(barrier, n + 1)

    sent = []

    def go(*args):
        c = copy(*args)
        c.start()
        sent.append(c)
        return c

    def landed(dst, recv):
        copy(dst, dst, recv, recv, sib).wait_recv()

    thin = send_ref.shape[2] // 2
    width = send_ref.shape[3]
    virt = w_ref.shape[1] // width

    def meta_copy(d):
        to = peer_at(d)
        return copy(
            meta_ref.at[to], picks_ref.at[pair], s_m.at[d], r_m.at[d], {"pair": to}
        )

    def out_copy(h, d):
        to = peer_at(d)
        return copy(
            send_ref.at[to, :, h * thin : (h + 1) * thin, :], got_ref.at[h, pair], s_a.at[h, d],
            r_a.at[h, d], {"pair": to},
        )

    def back_copy(h, d):
        to = peer_at(d)
        return copy(bsend.at[h, to], bgot.at[h, pair], s_b.at[h, d], r_b.at[h, d], {"pair": to})

    def each_peer(act):
        def one(d, carry):
            act(d)
            return carry

        lax.fori_loop(1, n, one, 0)

    def first(d):
        meta_copy(d).start()
        out_copy(0, d).start()

    each_peer(first)
    each_peer(lambda d: out_copy(1, d).start())
    picks_ref[pair] = meta_ref[pair]
    for h in range(2):
        got_ref[h, pair] = send_ref[pair, :, h * thin : (h + 1) * thin, :]
    step = 64 if f_ref.shape[0] % 64 == 0 else f_ref.shape[0]

    def flatten(i, carry):
        at_rows = pl.ds(pl.multiple_of(i * step, step), step)
        f_ref[at_rows, :] = factor_ref[at_rows].astype(F32).reshape(step, -1).astype(BF16)
        return carry

    lax.fori_loop(0, f_ref.shape[0] // step, flatten, 0)

    def combine(h):
        total = 0.0
        for r in range(CAP):
            rows_r = got_ref[h, :, r].astype(F32).reshape(n, thin * width).astype(BF16)
            total = total + lax.dot_general(
                picks_ref[:, r, :].astype(BF16), rows_r, TN, preferred_element_type=F32
            )
        total = total[: virt * virt].reshape(virt * virt, thin, width).astype(BF16)
        for a in range(virt):
            for c in range(virt):
                low = h * half + a * thin
                w_ref[low : low + thin, c * width : (c + 1) * width] = total[a * virt + c]
        piece = slice(h * half, (h + 1) * half)
        go(w_ref.at[piece], wall.at[0, piece], s_w.at[2 * h], r_w.at[2 * h], right)
        go(w_ref.at[piece], wall.at[1, piece], s_w.at[2 * h + 1], r_w.at[2 * h + 1], left)

    each_peer(lambda d: meta_copy(d).wait_recv())
    each_peer(lambda d: out_copy(0, d).wait_recv())
    combine(0)
    landed(wall.at[0, :half], r_w.at[0])
    go(wall.at[0, :half], wall.at[2, :half], s_w.at[4], r_w.at[4], right)
    each_peer(lambda d: out_copy(1, d).wait_recv())
    combine(1)

    own = pl.multiple_of(core * half, half)
    other = pl.multiple_of((1 - core) * half, half)

    def weights_product(t):
        if t == 0:
            landed(wall.at[1, half:], r_w.at[3])
            go(wall.at[1, half:], wall.at[2, half:], s_w.at[5], r_w.at[5], left)
            landed(wall.at[0, half:], r_w.at[2])
        if t == 1:
            landed(wall.at[1, :half], r_w.at[1])
        if t == 2:
            landed(wall.at[2, :half], r_w.at[4])
            landed(wall.at[2, half:], r_w.at[5])
        w = w_ref if t == 3 else wall.at[t]
        w_both = jnp.concatenate([w[pl.ds(other, half), :], w[pl.ds(own, half), :]], axis=0)

        def block(b, carry):
            got = lax.dot_general(
                w_both, f_ref[pl.ds(pl.multiple_of(b * cols, cols), cols), :], NT,
                preferred_element_type=F32,
            )
            sibtx[t, b] = got[:half]
            part[t, b] = got[half:]
            return carry

        lax.fori_loop(0, NY, block, 0)
        go(sibtx.at[t], sibrx.at[t], s_sib.at[t], r_sib.at[t], sib)

    def core_sum(t):
        landed(sibrx.at[t], r_sib.at[t])

        def block(b, carry):
            part[t, b] = part[t, b] + sibrx[t, b]
            return carry

        lax.fori_loop(0, NY, block, 0)
        ytx1[t] = part[t, lax.rem(y + 2, NY)].astype(BF16)
        go(ytx1.at[t, :mid], yrx1.at[t, 0], s_y1.at[t, 0], r_y1.at[t, 0], up)
        go(ytx1.at[t, mid:], yrx1.at[t, 1], s_y1.at[t, 1], r_y1.at[t, 1], down)

    def y_relay_sum(t):
        above, below = lax.rem(y + 1, NY), lax.rem(y + NY - 1, NY)
        landed(yrx1.at[t, 0], r_y1.at[t, 0])
        ytx2[t, 0, :mid] = (part[t, above, :mid] + yrx1[t, 0].astype(F32)).astype(BF16)
        ytx2[t, 0, mid:] = part[t, above, mid:].astype(BF16)
        go(ytx2.at[t, 0], yrx2.at[t, 0], s_y2.at[t, 0], r_y2.at[t, 0], up)
        landed(yrx1.at[t, 1], r_y1.at[t, 1])
        ytx2[t, 1, :mid] = part[t, below, :mid].astype(BF16)
        ytx2[t, 1, mid:] = (part[t, below, mid:] + yrx1[t, 1].astype(F32)).astype(BF16)
        go(ytx2.at[t, 1], yrx2.at[t, 1], s_y2.at[t, 1], r_y2.at[t, 1], down)

    def z_copy(t, d):
        to = lax.rem(z + d, nz)
        return copy(ztx.at[t, to], zrx.at[t, d], s_z.at[t, d], r_z.at[t, d], at(y, z + d, core))

    def y_sum(t):
        landed(yrx2.at[t, 0], r_y2.at[t, 0])
        landed(yrx2.at[t, 1], r_y2.at[t, 1])
        total = part[t, y] + yrx2[t, 0].astype(F32) + yrx2[t, 1].astype(F32)
        ztx[t] = total.reshape(nz, seg, cols).astype(BF16)

        def send(d, carry):
            z_copy(t, d).start()
            return carry

        lax.fori_loop(1, nz, send, 0)

    def g_copy(t, d):
        mine = xt.at[t, y, pl.ds(pl.multiple_of(core * half + z * seg, seg), seg), :]
        return copy(mine, mine, s_gz.at[t, d], r_gz.at[t, d], at(y, z + d, core))

    def z_sum(t):
        def add(d, total):
            landed(zrx.at[t, d], r_z.at[t, d])
            return total + zrx[t, d].astype(F32)

        total = lax.fori_loop(1, nz, add, ztx[t, z].astype(F32))
        xt[t, y, pl.ds(pl.multiple_of(core * half + z * seg, seg), seg), :] = total.astype(BF16)

        def send(d, carry):
            g_copy(t, d).start()
            return carry

        lax.fori_loop(1, nz, send, 0)

    def half_of(t, y_, start, size):
        first = pl.multiple_of(core * half + start, mid)
        return xt.at[t, lax.rem(y_ + NY, NY), pl.ds(first, size), :]

    def z_gather(t):
        def wait(d, carry):
            g_copy(t, d).wait_recv()
            return carry

        lax.fori_loop(1, nz, wait, 0)
        mine = half_of(t, y, 0, half)
        go(mine, mine, s_gy.at[t, 0], r_gy.at[t, 0], up)
        go(mine, mine, s_gy.at[t, 1], r_gy.at[t, 1], down)
        go(mine, mine, s_gs.at[t, 0], r_gs.at[t, 0], sib)

    def y_gather(t):
        landed(half_of(t, y - 1, 0, half), r_gy.at[t, 0])
        piece = half_of(t, y - 1, 0, mid)
        go(piece, piece, s_gy.at[t, 2], r_gy.at[t, 2], up)
        landed(half_of(t, y + 1, 0, half), r_gy.at[t, 1])
        piece = half_of(t, y + 1, mid, mid)
        go(piece, piece, s_gy.at[t, 3], r_gy.at[t, 3], down)
        for k, d in ((1, -1), (2, 1)):
            piece = half_of(t, y + d, 0, half)
            go(piece, piece, s_gs.at[t, k], r_gs.at[t, k], sib)

    def y_relay_gather(t):
        landed(half_of(t, y + 2, 0, mid), r_gy.at[t, 2])
        landed(half_of(t, y + 2, mid, mid), r_gy.at[t, 3])
        piece = half_of(t, y + 2, 0, half)
        go(piece, piece, s_gs.at[t, 3], r_gs.at[t, 3], sib)

    def block_product(t):
        for k in range(4):
            landed(half_of(t, y, 0, half), r_gs.at[t, k])

        def block(b, carry):
            got = jnp.dot(
                xt[t, b], f_ref[pl.ds(pl.multiple_of(b * cols, cols), cols), :],
                preferred_element_type=F32,
            )
            acc[t // 3] = jnp.where(b == 0, got, acc[t // 3] + got)
            return carry

        if t == 3:
            landed(relay.at[0], r_p.at[2])
            go(relay.at[0], prx.at[2, :half], s_p.at[4], r_p.at[4], right)
            landed(relay.at[1], r_p.at[3])
            go(relay.at[1], prx.at[2, half:], s_p.at[5], r_p.at[5], left)
        lax.fori_loop(0, NY, block, 0)
        if t < 3:
            ptx[t] = acc[0].astype(BF16)
        if t == 0:
            go(ptx.at[0], prx.at[1], s_p.at[1], r_p.at[1], left)
        if t == 1:
            go(ptx.at[1], prx.at[0], s_p.at[0], r_p.at[0], right)
        if t == 2:
            go(ptx.at[2, :half], relay.at[0], s_p.at[2], r_p.at[2], right)
            go(ptx.at[2, half:], relay.at[1], s_p.at[3], r_p.at[3], left)

    stages = (
        weights_product, core_sum, y_relay_sum, y_sum, z_sum, z_gather, y_gather, y_relay_gather, block_product,
    )
    for step in range(len(stages) + nx - 1):
        for k in reversed(range(len(stages))):
            if 0 <= step - k < nx:
                stages[k](step - k)

    landed(prx.at[0], r_p.at[0])
    landed(prx.at[1], r_p.at[1])
    for h in range(2):
        piece = slice(h * half, (h + 1) * half)
        landed(prx.at[2, piece], r_p.at[4 + h])
        total = acc[1, piece]
        for source in range(3):
            total = total + prx[source, piece].astype(F32)
        blocks = [
            total[a * thin : (a + 1) * thin, c * width : (c + 1) * width][None]
            for a in range(virt)
            for c in range(virt)
        ]
        flat = jnp.concatenate(blocks, axis=0).reshape(virt * virt, thin * width).astype(BF16)
        for r in range(CAP):
            chosen = picks_ref[:, r, :][:, : virt * virt].astype(BF16)
            got = jnp.dot(chosen, flat, preferred_element_type=F32)
            bsend[h, :, r] = got.reshape(n, thin, width).astype(BF16)
        each_peer(lambda d, h=h: back_copy(h, d).start())
        bgot[h, pair] = bsend[h, pair]

    count = out_ref.shape[0]
    few = count // 2

    def spot(who, h, first_block):
        low = lax.rem(who + nx, nx) * (2 * thin) + h * thin
        return out_ref.at[pl.ds(first_block, few), pl.ds(pl.multiple_of(low, thin), thin), :]

    for h in range(2):
        each_peer(lambda d, h=h: back_copy(h, d).wait_recv())
        total = 0.0
        for r in range(CAP):
            rows_r = bgot[h, :, r].astype(F32).reshape(n, thin * width).astype(BF16)
            total = total + jnp.dot(place_ref[r], rows_r, preferred_element_type=F32)
        low = pl.multiple_of(aux * (2 * thin) + h * thin, thin)
        out_ref[:, pl.ds(low, thin), :] = total.reshape(count, thin, width).astype(BF16)
        for q, to in enumerate((right, left)):
            for b in range(2):
                mine = spot(aux, h, (b ^ q) * few)
                m = 2 * q + b
                go(mine, mine, s_j.at[h, m], r_j.at[h, m], to)
    for h in range(2):
        from_left, from_right = spot(aux - 1, h, 0), spot(aux + 1, h, few)
        landed(from_left, r_j.at[h, 0])
        go(from_left, from_left, s_j.at[h, 4], r_j.at[h, 4], right)
        landed(from_right, r_j.at[h, 2])
        go(from_right, from_right, s_j.at[h, 5], r_j.at[h, 5], left)
    for h in range(2):
        landed(spot(aux - 1, h, few), r_j.at[h, 1])
        landed(spot(aux + 1, h, 0), r_j.at[h, 3])
        landed(spot(aux + 2, h, 0), r_j.at[h, 4])
        landed(spot(aux + 2, h, few), r_j.at[h, 5])

    def drained(d):
        meta_copy(d).wait_send()
        for h in range(2):
            out_copy(h, d).wait_send()
            back_copy(h, d).wait_send()

    each_peer(drained)
    for c in sent:
        c.wait_send()
    for t in range(nx):
        def drain(d, carry, t=t):
            z_copy(t, d).wait_send()
            g_copy(t, d).wait_send()
            return carry

        lax.fori_loop(1, nz, drain, 0)


def cycle(factors, send, meta, place):
    n, _, part, width = send.shape
    nx = lax.axis_size("aux")
    nz = n // (2 * NY)
    share_rows, virt, _ = factors.shape
    rows, flat = virt * part, virt * width
    half, cols = rows // 2, share_rows // NY
    seg, mid, thin = half // nz, half // 2, part // 2
    dma = pltpu.SemaphoreType.DMA
    vmem = pl.BlockSpec(memory_space=pltpu.VMEM)
    pairs = [
        (n,), (2, n), (2, n), (2, 6), (6,), (nx,), (nx, 2), (nx, 2), (nx, nz), (nx, nz), (nx, 4),
        (nx, 4), (6,),
    ]
    return pl.pallas_call(
        functools.partial(cycle_kernel, nz, nx),
        out_shape=jax.ShapeDtypeStruct((place.shape[1], nx * part, width), BF16),
        in_specs=[vmem] * 4,
        out_specs=vmem,
        scratch_shapes=[
            pltpu.VMEM((share_rows, flat), BF16),
            pltpu.VMEM((2, n, CAP, thin, width), BF16),
            pltpu.VMEM(meta.shape, F32),
            pltpu.VMEM((2, n, CAP, thin, width), BF16),
            pltpu.VMEM((2, n, CAP, thin, width), BF16),
            pltpu.VMEM((rows, flat), BF16),
            pltpu.VMEM((3, rows, flat), BF16),
            pltpu.VMEM((nx, NY, half, cols), F32),
            pltpu.VMEM((nx, NY, half, cols), F32),
            pltpu.VMEM((nx, NY, half, cols), F32),
            pltpu.VMEM((nx, half, cols), BF16),
            pltpu.VMEM((nx, 2, mid, cols), BF16),
            pltpu.VMEM((nx, 2, half, cols), BF16),
            pltpu.VMEM((nx, 2, half, cols), BF16),
            pltpu.VMEM((nx, nz, seg, cols), BF16),
            pltpu.VMEM((nx, nz, seg, cols), BF16),
            pltpu.VMEM((nx, NY, rows, cols), BF16),
            pltpu.VMEM((3, rows, flat), BF16),
            pltpu.VMEM((3, rows, flat), BF16),
            pltpu.VMEM((2, half, flat), BF16),
            pltpu.VMEM((2, rows, flat), F32),
        ]
        + [dma(shape) for shape in pairs for _ in range(2)],
        compiler_params=pltpu.CompilerParams(
            collective_id=0, has_side_effects=True, vmem_limit_bytes=58 << 20
        ),
        cost_estimate=pl.CostEstimate(
            flops=4 * nx * rows * flat * share_rows, bytes_accessed=8 << 20, transcendentals=0
        ),
    )(factors, send, meta, place)


def on_device(factors, amplitudes, block_list, owner_map):
    pair_count = lax.axis_size("pair")
    aux_count = lax.axis_size("aux")
    share = lax.axis_index("aux")
    block_count, block_width, _ = amplitudes.shape
    virt = factors.shape[2]
    lanes = max(128, virt * virt)
    part = block_width // aux_count
    ids = lax.iota(jnp.int32, block_count)
    hits = block_list[:, 0][:, None] == lax.iota(jnp.int32, owner_map.shape[0])[None, :]
    owners = jnp.sum(jnp.where(hits, owner_map[None, :], 0), axis=1)
    combo = block_list[:, 1] * virt + block_list[:, 2]
    same = (owners[:, None] == owners[None, :]) & (ids[None, :] < ids[:, None])
    rank = jnp.sum(same.astype(jnp.int32), axis=1)
    slots = owners * CAP + rank
    placing = (slots[:, None] == lax.iota(jnp.int32, pair_count * CAP)[None, :]).astype(BF16)
    at_combo = (combo[:, None] == lax.iota(jnp.int32, lanes)[None, :]).astype(BF16)
    meta = jnp.einsum("js,jn->sn", placing, at_combo, preferred_element_type=F32)
    mine = lax.dynamic_slice_in_dim(amplitudes, share * part, part, axis=1)
    sent = jnp.einsum("js,jm->sm", placing, mine.reshape(block_count, -1), preferred_element_type=F32)
    to_owner = owners[:, None] == lax.iota(jnp.int32, pair_count)[None, :]
    place = jnp.stack([to_owner & (rank == r)[:, None] for r in range(CAP)]).astype(BF16)
    return cycle(
        factors.reshape(-1, virt, block_width),
        sent.astype(BF16).reshape(pair_count, CAP, part, block_width),
        meta.reshape(pair_count, CAP, lanes),
        place,
    )


def solution(mesh):
    placed = (P("pair", "aux", None, None), P("pair", None, None), P("pair", None), P())
    return jax.shard_map(
        on_device, mesh=mesh, in_specs=placed, out_specs=P("pair", None, None), check_vma=False
    )
```

time: 270 us -> 180 us (0.67)
  blocking collectives: 99.8 us -> 0 us
  Pallas kernels: 102 us -> 172 us
  waiting for transfers between devices: 25.1 us -> 0 us
  between operations: 13.5 us -> 0.05 us
  starting transfers between devices: 13.2 us -> 0 us
  local copies, waits for them, and re-layouts: 13.3 us -> 3.95 us
    pallas_call x1, Pallas kernels: 102 us -> 172 us  [cycle(): pl.pallas_call(functools.partial(cycle_kernel, nz, nx), out_shape=jax.Sha...]
    all_gather x1 -> x0, blocking collectives: 59.3 us -> none  [on_device(): all_codes = lax.all_gather(codes, 'pair', axis=0, tiled=False)]
    all_to_all x1 -> x0, blocking collectives: 40.5 us -> none  [on_device(): back = lax.all_to_all(back, 'pair', split_axis=0, concat_axis=0, tiled=True)]
    all_gather x1 -> x0, waiting for transfers between devices: 25.1 us -> none  [on_device(): return lax.all_gather(result, 'aux', axis=1, tiled=True)]
    all_to_all x1 -> x0, starting transfers between devices: 13.2 us -> none  [on_device(): got = lax.all_to_all(sent, 'pair', split_axis=0, concat_axis=0, tiled=True)]
    unnamed x11 -> x4, local copies, waits for them, and re-layouts: 12.2 us -> 3.92 us
  transfers between devices with their start and end apart: 2 -> 0, of which waited for: 1 -> 0; matrix products, arithmetic and copies ran while one was open for 2% -> 0% of each run, Pallas kernels for 0% -> 0%
where the time goes in v3:
time: 180 us
  Pallas kernels  172 us (96%)
  local copies, waits for them, and re-layouts  3.95 us (2%)
  other arithmetic  2.56 us (1%)
    pallas_call x1, Pallas kernels, cycle(): pl.pallas_call(functools.partial(cycle_kernel, nz, nx), out_shape=jax.Sha...  172 us
    unnamed x4, local copies, waits for them, and re-layouts  3.92 us

profile of v3, /device:TPU:1, one launch (start us, length us, event | category | flops | bytes accessed | tf_op | source)
XLA Modules:
  0.0 179.7 jit_solution(9542614282978245655)
XLA Ops:
  0.0 0.0 copy-start
  0.0 0.8 add_bitcast_fusion
  0.8 0.8 select_reduce_fusion
  1.7 0.2 convert_reduce_fusion
  1.9 0.1 fusion.4
  2.0 0.6 add_convert_fusion.place_ref
  2.6 0.9 fusion.5
  3.5 0.0 copy-done
  3.5 0.5 fusion
  4.1 1.2 copy.6
  5.3 171.7 %shard_map.46 = bf16[48,128,128]{2,1,0:T(8,128)(2,1)} custom-call(bf16[2048,8,128]{2,1,0:T(8,128)(2,1)} %bitcast.16, bf16[64,2,32,128]{3,2,1,0:T(8,128)(2,1)} %bitcast.15, f32[64,2,128]{2,1,0:T(2,128)} %bitcast.17, bf16[2,48,64]{2,1,0:T(8,128)(2,1)} %add_convert_fusion.place_ref), custom_call_target="tpu_custom_call" | custom-call | flops 8589934592 | bytes 8388608 | tf_op jit(solution)/shard_map/pallas_call | solution.py:381
  177.0 2.7 %copy.12 = bf16[48,128,128]{2,1,0:T(8,128)(2,1)} copy(bf16[48,128,128]{2,1,0:T(8,128)(2,1)} %shard_map.46) | data formatting | bytes 3145728
  (3 shorter events, 0.0 us)
Async XLA Ops:
  0.0 3.5 %copy-start = (bf16[48,128,128]{2,1,0:T(8,128)(2,1)S(1)}, bf16[48,128,128]{2,1,0:T(8,128)(2,1)}, u32[]{:S(2)}) copy-start(bf16[48,128,128]{2,1,0:T(8,128)(2,1)} %param.5) | copy-start | bytes 4718596

commit v4 on v3

--- a/solution.py
+++ b/solution.py
@@ -77,19 +77,19 @@
     def meta_copy(d):
         to = peer_at(d)
         return copy(
-            meta_ref.at[to], picks_ref.at[pair], s_m.at[d], r_m.at[d], {"pair": to}
+            meta_ref.at[to], picks_ref.at[pair], s_m.at[0], r_m.at[0], {"pair": to}
         )
 
     def out_copy(h, d):
         to = peer_at(d)
         return copy(
-            send_ref.at[to, :, h * thin : (h + 1) * thin, :], got_ref.at[h, pair], s_a.at[h, d],
-            r_a.at[h, d], {"pair": to},
+            send_ref.at[to, :, h * thin : (h + 1) * thin, :], got_ref.at[h, pair], s_a.at[h],
+            r_a.at[h], {"pair": to},
         )
 
     def back_copy(h, d):
         to = peer_at(d)
-        return copy(bsend.at[h, to], bgot.at[h, pair], s_b.at[h, d], r_b.at[h, d], {"pair": to})
+        return copy(bsend.at[h, to], bgot.at[h, pair], s_b.at[h], r_b.at[h], {"pair": to})
 
     def each_peer(act):
         def one(d, carry):
@@ -132,12 +132,12 @@
         go(w_ref.at[piece], wall.at[0, piece], s_w.at[2 * h], r_w.at[2 * h], right)
         go(w_ref.at[piece], wall.at[1, piece], s_w.at[2 * h + 1], r_w.at[2 * h + 1], left)
 
-    each_peer(lambda d: meta_copy(d).wait_recv())
-    each_peer(lambda d: out_copy(0, d).wait_recv())
+    landed(picks_ref.at[: n - 1], r_m.at[0])
+    landed(got_ref.at[0, : n - 1], r_a.at[0])
     combine(0)
     landed(wall.at[0, :half], r_w.at[0])
     go(wall.at[0, :half], wall.at[2, :half], s_w.at[4], r_w.at[4], right)
-    each_peer(lambda d: out_copy(1, d).wait_recv())
+    landed(got_ref.at[1, : n - 1], r_a.at[1])
     combine(1)
 
     own = pl.multiple_of(core * half, half)
@@ -193,7 +193,7 @@
 
     def z_copy(t, d):
         to = lax.rem(z + d, nz)
-        return copy(ztx.at[t, to], zrx.at[t, d], s_z.at[t, d], r_z.at[t, d], at(y, z + d, core))
+        return copy(ztx.at[t, to], zrx.at[t, d], s_z.at[t], r_z.at[t], at(y, z + d, core))
 
     def y_sum(t):
         landed(yrx2.at[t, 0], r_y2.at[t, 0])
@@ -209,11 +209,12 @@
 
     def g_copy(t, d):
         mine = xt.at[t, y, pl.ds(pl.multiple_of(core * half + z * seg, seg), seg), :]
-        return copy(mine, mine, s_gz.at[t, d], r_gz.at[t, d], at(y, z + d, core))
+        return copy(mine, mine, s_gz.at[t], r_gz.at[t], at(y, z + d, core))
 
     def z_sum(t):
+        landed(zrx.at[t, 1:], r_z.at[t])
+
         def add(d, total):
-            landed(zrx.at[t, d], r_z.at[t, d])
             return total + zrx[t, d].astype(F32)
 
         total = lax.fori_loop(1, nz, add, ztx[t, z].astype(F32))
@@ -230,11 +231,7 @@
         return xt.at[t, lax.rem(y_ + NY, NY), pl.ds(first, size), :]
 
     def z_gather(t):
-        def wait(d, carry):
-            g_copy(t, d).wait_recv()
-            return carry
-
-        lax.fori_loop(1, nz, wait, 0)
+        landed(zrx.at[t, 1:], r_gz.at[t])
         mine = half_of(t, y, 0, half)
         go(mine, mine, s_gy.at[t, 0], r_gy.at[t, 0], up)
         go(mine, mine, s_gy.at[t, 1], r_gy.at[t, 1], down)
@@ -322,7 +319,7 @@
         return out_ref.at[pl.ds(first_block, few), pl.ds(pl.multiple_of(low, thin), thin), :]
 
     for h in range(2):
-        each_peer(lambda d, h=h: back_copy(h, d).wait_recv())
+        landed(bgot.at[h, : n - 1], r_b.at[h])
         total = 0.0
         for r in range(CAP):
             rows_r = bgot[h, :, r].astype(F32).reshape(n, thin * width).astype(BF16)
@@ -346,22 +343,18 @@
         landed(spot(aux + 2, h, 0), r_j.at[h, 4])
         landed(spot(aux + 2, h, few), r_j.at[h, 5])
 
-    def drained(d):
-        meta_copy(d).wait_send()
-        for h in range(2):
-            out_copy(h, d).wait_send()
-            back_copy(h, d).wait_send()
-
-    each_peer(drained)
+    def left_here(src, send):
+        copy(src, src, send, send, sib).wait_send()
+
+    left_here(picks_ref.at[: n - 1], s_m.at[0])
+    for h in range(2):
+        left_here(got_ref.at[h, : n - 1], s_a.at[h])
+        left_here(bgot.at[h, : n - 1], s_b.at[h])
     for c in sent:
         c.wait_send()
     for t in range(nx):
-        def drain(d, carry, t=t):
-            z_copy(t, d).wait_send()
-            g_copy(t, d).wait_send()
-            return carry
-
-        lax.fori_loop(1, nz, drain, 0)
+        left_here(zrx.at[t, 1:], s_z.at[t])
+        left_here(zrx.at[t, 1:], s_gz.at[t])
 
 
 def cycle(factors, send, meta, place):
@@ -375,8 +368,8 @@
     dma = pltpu.SemaphoreType.DMA
     vmem = pl.BlockSpec(memory_space=pltpu.VMEM)
     pairs = [
-        (n,), (2, n), (2, n), (2, 6), (6,), (nx,), (nx, 2), (nx, 2), (nx, nz), (nx, nz), (nx, 4),
-        (nx, 4), (6,),
+        (1,), (2,), (2,), (2, 6), (6,), (nx,), (nx, 2), (nx, 2), (nx,), (nx,), (nx, 4), (nx, 4),
+        (6,),
     ]
     return pl.pallas_call(
         functools.partial(cycle_kernel, nz, nx),
@@ -408,7 +401,7 @@
         ]
         + [dma(shape) for shape in pairs for _ in range(2)],
         compiler_params=pltpu.CompilerParams(
-            collective_id=0, has_side_effects=True, vmem_limit_bytes=58 << 20
+            collective_id=0, has_side_effects=True, vmem_limit_bytes=46 << 20
         ),
         cost_estimate=pl.CostEstimate(
             flops=4 * nx * rows * flat * share_rows, bytes_accessed=8 << 20, transcendentals=0

time: 180 us -> 167 us (0.928)
  Pallas kernels: 172 us -> 160 us
    pallas_call x1, Pallas kernels: 172 us -> 160 us  [cycle(): pl.pallas_call(functools.partial(cycle_kernel, nz, nx), out_shape=jax.Sha...]
    unnamed x4 -> x6, local copies, waits for them, and re-layouts: 3.92 us -> 2.73 us
where the time goes in v4:
time: 167 us; the launch traced here: 166 us
  Pallas kernels  160 us (96%)
  local copies, waits for them, and re-layouts  2.77 us (2%)
  other arithmetic  1.96 us (1%)
    pallas_call x1, Pallas kernels, cycle(): pl.pallas_call(functools.partial(cycle_kernel, nz, nx), out_shape=jax.Sha...  160 us

profile of v4, /device:TPU:1, one launch (start us, length us, event | category | flops | bytes accessed | tf_op | source)
XLA Modules:
  0.0 166.0 jit_solution(5907419635467419724)
XLA Ops:
  0.0 0.0 copy-start
  0.0 0.8 add_bitcast_fusion
  0.8 0.8 select_reduce_fusion
  1.7 0.2 convert_reduce_fusion
  1.9 0.1 fusion.4
  2.0 0.3 fusion.5
  2.3 0.0 copy-done
  2.3 0.0 copy-start.1
  2.3 0.5 fusion
  2.9 0.2 copy.6
  3.1 1.3 copy-done.1
  4.5 160.3 %shard_map.46 = bf16[48,128,128]{2,1,0:T(8,128)(2,1)S(1)} custom-call(bf16[2048,8,128]{2,1,0:T(8,128)(2,1)S(1)} %bitcast.15, bf16[64,2,32,128]{3,2,1,0:T(8,128)(2,1)S(1)} %bitcast.14, f32[64,2,128]{2,1,0:T(2,128)S(1)} %bitcast.16, bf16[2,48,64]{2,1,0:T(8,128)(2,1)S(1)} %add_convert_fusion.place_ref), custom_call_target="tpu_custom_call" | custom-call | flops 8589934592 | bytes 8388608 | tf_op jit(solution)/shard_map/pallas_call | solution.py:374
  164.8 1.1 copy.12
  (4 shorter events, 0.1 us)
Async XLA Ops:
  0.0 2.3 %copy-start = (bf16[48,128,128]{2,1,0:T(8,128)(2,1)S(1)}, bf16[48,128,128]{2,1,0:T(8,128)(2,1)}, u32[]{:S(2)}) copy-start(bf16[48,128,128]{2,1,0:T(8,128)(2,1)} %param.5) | copy-start | bytes 4718596
  2.3 2.2 %copy-start.1 = (bf16[1,2048,8,128]{3,2,1,0:T(8,128)(2,1)S(1)}, bf16[1,2048,8,128]{3,2,1,0:T(8,128)(2,1)}, u32[]{:S(2)}) copy-start(bf16[1,2048,8,128]{3,2,1,0:T(8,128)(2,1)} %param.4) | copy-start | bytes 12582916

commit v5 on v4

--- a/solution.py
+++ b/solution.py
@@ -8,6 +8,7 @@
 from jax.sharding import PartitionSpec as P
 
 CAP = 2
+ORDER = ((3, 0), (0, 0), (1, 0), (2, 0), (0, 1), (1, 1), (2, 1), (3, 1))
 NY = 4
 F32 = jnp.float32
 BF16 = jnp.bfloat16
@@ -18,7 +19,7 @@
 
 def cycle_kernel(
     nz, nx, factor_ref, send_ref, meta_ref, place_ref, out_ref, f_ref, got_ref, picks_ref, bsend,
-    bgot, w_ref, wall, sibtx, sibrx, part, ytx1, yrx1, ytx2, yrx2, ztx, zrx, xt, ptx, prx, relay,
+    bgot, w_ref, wall, sibtx, sibrx, part, ytx1, yrx1, ytx2, yrx2, ztx, zrx, zg, xt, ptx, prx, relay,
     acc, s_m, r_m, s_a, r_a, s_b, r_b, s_j, r_j, s_w, r_w, s_sib, r_sib, s_y1, r_y1, s_y2, r_y2,
     s_z, r_z, s_gz, r_gz, s_gy, r_gy, s_gs, r_gs, s_p, r_p,
 ):
@@ -29,6 +30,7 @@
     mid = half // 2
     cols = part.shape[3]
     rows = 2 * half
+    chunks = len(ORDER)
 
     def at(y_, z_, c_):
         return {"pair": (lax.rem(y_ + NY, NY) * nz + lax.rem(z_ + nz, nz)) * 2 + c_}
@@ -126,34 +128,32 @@
         total = total[: virt * virt].reshape(virt * virt, thin, width).astype(BF16)
         for a in range(virt):
             for c in range(virt):
-                low = h * half + a * thin
+                low = h * rows + a * thin
                 w_ref[low : low + thin, c * width : (c + 1) * width] = total[a * virt + c]
-        piece = slice(h * half, (h + 1) * half)
-        go(w_ref.at[piece], wall.at[0, piece], s_w.at[2 * h], r_w.at[2 * h], right)
-        go(w_ref.at[piece], wall.at[1, piece], s_w.at[2 * h + 1], r_w.at[2 * h + 1], left)
+        piece = slice(h * rows, (h + 1) * rows)
+        go(w_ref.at[piece], wall.at[0, piece], s_w.at[h, 0], r_w.at[h, 0], right)
+        go(w_ref.at[piece], wall.at[1, piece], s_w.at[h, 1], r_w.at[h, 1], left)
 
     landed(picks_ref.at[: n - 1], r_m.at[0])
     landed(got_ref.at[0, : n - 1], r_a.at[0])
     combine(0)
-    landed(wall.at[0, :half], r_w.at[0])
-    go(wall.at[0, :half], wall.at[2, :half], s_w.at[4], r_w.at[4], right)
-    landed(got_ref.at[1, : n - 1], r_a.at[1])
-    combine(1)
 
     own = pl.multiple_of(core * half, half)
     other = pl.multiple_of((1 - core) * half, half)
 
     def weights_product(t):
-        if t == 0:
-            landed(wall.at[1, half:], r_w.at[3])
-            go(wall.at[1, half:], wall.at[2, half:], s_w.at[5], r_w.at[5], left)
-            landed(wall.at[0, half:], r_w.at[2])
-        if t == 1:
-            landed(wall.at[1, :half], r_w.at[1])
-        if t == 2:
-            landed(wall.at[2, :half], r_w.at[4])
-            landed(wall.at[2, half:], r_w.at[5])
-        w = w_ref if t == 3 else wall.at[t]
+        share, h = ORDER[t]
+        piece = slice(h * rows, (h + 1) * rows)
+        low, high = slice(h * rows, h * rows + half), slice(h * rows + half, (h + 1) * rows)
+        if share == 0:
+            landed(wall.at[0, piece], r_w.at[h, 0])
+            go(wall.at[0, low], wall.at[2, low], s_w.at[h, 2], r_w.at[h, 2], right)
+            landed(wall.at[1, piece], r_w.at[h, 1])
+            go(wall.at[1, high], wall.at[2, high], s_w.at[h, 3], r_w.at[h, 3], left)
+        if share == 2:
+            landed(wall.at[2, low], r_w.at[h, 2])
+            landed(wall.at[2, high], r_w.at[h, 3])
+        w = (w_ref if share == 3 else wall.at[share]).at[piece]
         w_both = jnp.concatenate([w[pl.ds(other, half), :], w[pl.ds(own, half), :]], axis=0)
 
         def block(b, carry):
@@ -208,7 +208,7 @@
         lax.fori_loop(1, nz, send, 0)
 
     def g_copy(t, d):
-        mine = xt.at[t, y, pl.ds(pl.multiple_of(core * half + z * seg, seg), seg), :]
+        mine = zg.at[t, z]
         return copy(mine, mine, s_gz.at[t], r_gz.at[t], at(y, z + d, core))
 
     def z_sum(t):
@@ -218,7 +218,7 @@
             return total + zrx[t, d].astype(F32)
 
         total = lax.fori_loop(1, nz, add, ztx[t, z].astype(F32))
-        xt[t, y, pl.ds(pl.multiple_of(core * half + z * seg, seg), seg), :] = total.astype(BF16)
+        zg[t, z] = total.astype(BF16)
 
         def send(d, carry):
             g_copy(t, d).start()
@@ -232,6 +232,8 @@
 
     def z_gather(t):
         landed(zrx.at[t, 1:], r_gz.at[t])
+        joined = zg[t].astype(F32).reshape(half, cols).astype(BF16)
+        xt[t, y, pl.ds(pl.multiple_of(core * half, half), half), :] = joined
         mine = half_of(t, y, 0, half)
         go(mine, mine, s_gy.at[t, 0], r_gy.at[t, 0], up)
         go(mine, mine, s_gy.at[t, 1], r_gy.at[t, 1], down)
@@ -258,44 +260,45 @@
         for k in range(4):
             landed(half_of(t, y, 0, half), r_gs.at[t, k])
 
+        share, h = ORDER[t]
+        piece = slice(h * rows, (h + 1) * rows)
+        k = 1 + h if share == 3 else 0
+
         def block(b, carry):
             got = jnp.dot(
                 xt[t, b], f_ref[pl.ds(pl.multiple_of(b * cols, cols), cols), :],
                 preferred_element_type=F32,
             )
-            acc[t // 3] = jnp.where(b == 0, got, acc[t // 3] + got)
-            return carry
-
-        if t == 3:
-            landed(relay.at[0], r_p.at[2])
-            go(relay.at[0], prx.at[2, :half], s_p.at[4], r_p.at[4], right)
-            landed(relay.at[1], r_p.at[3])
-            go(relay.at[1], prx.at[2, half:], s_p.at[5], r_p.at[5], left)
+            acc[k] = jnp.where(b == 0, got, acc[k] + got)
+            return carry
+
+        if t and ORDER[t - 1][0] == 2:
+            g = ORDER[t - 1][1]
+            low, high = slice(g * rows, g * rows + half), slice(g * rows + half, (g + 1) * rows)
+            landed(relay.at[g, 0], r_p.at[g, 2])
+            go(relay.at[g, 0], prx.at[2, low], s_p.at[g, 4], r_p.at[g, 4], right)
+            landed(relay.at[g, 1], r_p.at[g, 3])
+            go(relay.at[g, 1], prx.at[2, high], s_p.at[g, 5], r_p.at[g, 5], left)
         lax.fori_loop(0, NY, block, 0)
-        if t < 3:
-            ptx[t] = acc[0].astype(BF16)
-        if t == 0:
-            go(ptx.at[0], prx.at[1], s_p.at[1], r_p.at[1], left)
-        if t == 1:
-            go(ptx.at[1], prx.at[0], s_p.at[0], r_p.at[0], right)
-        if t == 2:
-            go(ptx.at[2, :half], relay.at[0], s_p.at[2], r_p.at[2], right)
-            go(ptx.at[2, half:], relay.at[1], s_p.at[3], r_p.at[3], left)
+        if share < 3:
+            ptx[share, piece] = acc[0].astype(BF16)
+        if share == 0:
+            go(ptx.at[0, piece], prx.at[1, piece], s_p.at[h, 1], r_p.at[h, 1], left)
+        if share == 1:
+            go(ptx.at[1, piece], prx.at[0, piece], s_p.at[h, 0], r_p.at[h, 0], right)
+        if share == 2:
+            low, high = slice(h * rows, h * rows + half), slice(h * rows + half, (h + 1) * rows)
+            go(ptx.at[2, low], relay.at[h, 0], s_p.at[h, 2], r_p.at[h, 2], right)
+            go(ptx.at[2, high], relay.at[h, 1], s_p.at[h, 3], r_p.at[h, 3], left)
 
     stages = (
         weights_product, core_sum, y_relay_sum, y_sum, z_sum, z_gather, y_gather, y_relay_gather, block_product,
     )
-    for step in range(len(stages) + nx - 1):
-        for k in reversed(range(len(stages))):
-            if 0 <= step - k < nx:
-                stages[k](step - k)
-
-    landed(prx.at[0], r_p.at[0])
-    landed(prx.at[1], r_p.at[1])
-    for h in range(2):
-        piece = slice(h * half, (h + 1) * half)
-        landed(prx.at[2, piece], r_p.at[4 + h])
-        total = acc[1, piece]
+    def give_back(h):
+        piece = slice(h * rows, (h + 1) * rows)
+        for k in (0, 1, 4, 5):
+            landed(prx.at[min(k, 2), piece if k < 2 else slice(half)], r_p.at[h, k])
+        total = acc[1 + h]
         for source in range(3):
             total = total + prx[source, piece].astype(F32)
         blocks = [
@@ -308,8 +311,19 @@
             chosen = picks_ref[:, r, :][:, : virt * virt].astype(BF16)
             got = jnp.dot(chosen, flat, preferred_element_type=F32)
             bsend[h, :, r] = got.reshape(n, thin, width).astype(BF16)
-        each_peer(lambda d, h=h: back_copy(h, d).start())
+        each_peer(lambda d: back_copy(h, d).start())
         bgot[h, pair] = bsend[h, pair]
+
+    for step in range(len(stages) + chunks - 1):
+        if step == 3:
+            landed(got_ref.at[1, : n - 1], r_a.at[1])
+            combine(1)
+        if step == 14:
+            give_back(0)
+        for k in reversed(range(len(stages))):
+            if 0 <= step - k < chunks:
+                stages[k](step - k)
+    give_back(1)
 
     count = out_ref.shape[0]
     few = count // 2
@@ -352,7 +366,7 @@
         left_here(bgot.at[h, : n - 1], s_b.at[h])
     for c in sent:
         c.wait_send()
-    for t in range(nx):
+    for t in range(chunks):
         left_here(zrx.at[t, 1:], s_z.at[t])
         left_here(zrx.at[t, 1:], s_gz.at[t])
 
@@ -363,13 +377,14 @@
     nz = n // (2 * NY)
     share_rows, virt, _ = factors.shape
     rows, flat = virt * part, virt * width
-    half, cols = rows // 2, share_rows // NY
+    half, cols = rows // 4, share_rows // NY
+    chunks = len(ORDER)
     seg, mid, thin = half // nz, half // 2, part // 2
     dma = pltpu.SemaphoreType.DMA
     vmem = pl.BlockSpec(memory_space=pltpu.VMEM)
     pairs = [
-        (1,), (2,), (2,), (2, 6), (6,), (nx,), (nx, 2), (nx, 2), (nx,), (nx,), (nx, 4), (nx, 4),
-        (6,),
+        (1,), (2,), (2,), (2, 6), (2, 4), (chunks,), (chunks, 2), (chunks, 2), (chunks,), (chunks,),
+        (chunks, 4), (chunks, 4), (2, 6),
     ]
     return pl.pallas_call(
         functools.partial(cycle_kernel, nz, nx),
@@ -384,20 +399,21 @@
             pltpu.VMEM((2, n, CAP, thin, width), BF16),
             pltpu.VMEM((rows, flat), BF16),
             pltpu.VMEM((3, rows, flat), BF16),
-            pltpu.VMEM((nx, NY, half, cols), F32),
-            pltpu.VMEM((nx, NY, half, cols), F32),
-            pltpu.VMEM((nx, NY, half, cols), F32),
-            pltpu.VMEM((nx, half, cols), BF16),
-            pltpu.VMEM((nx, 2, mid, cols), BF16),
-            pltpu.VMEM((nx, 2, half, cols), BF16),
-            pltpu.VMEM((nx, 2, half, cols), BF16),
-            pltpu.VMEM((nx, nz, seg, cols), BF16),
-            pltpu.VMEM((nx, nz, seg, cols), BF16),
-            pltpu.VMEM((nx, NY, rows, cols), BF16),
+            pltpu.VMEM((chunks, NY, half, cols), F32),
+            pltpu.VMEM((chunks, NY, half, cols), F32),
+            pltpu.VMEM((chunks, NY, half, cols), F32),
+            pltpu.VMEM((chunks, half, cols), BF16),
+            pltpu.VMEM((chunks, 2, mid, cols), BF16),
+            pltpu.VMEM((chunks, 2, half, cols), BF16),
+            pltpu.VMEM((chunks, 2, half, cols), BF16),
+            pltpu.VMEM((chunks, nz, seg, cols), BF16),
+            pltpu.VMEM((chunks, nz, seg, cols), BF16),
+            pltpu.VMEM((chunks, nz, seg, cols), BF16),
+            pltpu.VMEM((chunks, NY, 2 * half, cols), BF16),
             pltpu.VMEM((3, rows, flat), BF16),
             pltpu.VMEM((3, rows, flat), BF16),
-            pltpu.VMEM((2, half, flat), BF16),
-            pltpu.VMEM((2, rows, flat), F32),
+            pltpu.VMEM((2, 2, half, flat), BF16),
+            pltpu.VMEM((3, 2 * half, flat), F32),
         ]
         + [dma(shape) for shape in pairs for _ in range(2)],
         compiler_params=pltpu.CompilerParams(

time: 167 us -> 146 us (0.87)
  Pallas kernels: 160 us -> 141 us
    pallas_call x1, Pallas kernels: 160 us -> 141 us  [cycle(): pl.pallas_call(functools.partial(cycle_kernel, nz, nx), out_shape=jax.Sha...]
where the time goes in v5:
time: 146 us
  Pallas kernels  141 us (97%)
  local copies, waits for them, and re-layouts  2.77 us (2%)
  other arithmetic  1.96 us (1%)
    pallas_call x1, Pallas kernels, cycle(): pl.pallas_call(functools.partial(cycle_kernel, nz, nx), out_shape=jax.Sha...  141 us

profile of v5, /device:TPU:1, one launch (start us, length us, event | category | flops | bytes accessed | tf_op | source)
XLA Modules:
  0.0 146.3 jit_solution(12767237820441595751)
XLA Ops:
  0.0 0.0 copy-start
  0.0 0.8 add_bitcast_fusion
  0.8 0.8 select_reduce_fusion
  1.7 0.2 convert_reduce_fusion
  1.9 0.1 fusion.4
  2.0 0.3 fusion.5
  2.3 0.0 copy-done
  2.3 0.0 copy-start.1
  2.3 0.5 fusion
  2.9 0.2 copy.6
  3.1 1.3 copy-done.1
  4.5 140.7 %shard_map.46 = bf16[48,128,128]{2,1,0:T(8,128)(2,1)S(1)} custom-call(bf16[2048,8,128]{2,1,0:T(8,128)(2,1)S(1)} %bitcast.15, bf16[64,2,32,128]{3,2,1,0:T(8,128)(2,1)S(1)} %bitcast.14, f32[64,2,128]{2,1,0:T(2,128)S(1)} %bitcast.16, bf16[2,48,64]{2,1,0:T(8,128)(2,1)S(1)} %add_convert_fusion.place_ref), custom_call_target="tpu_custom_call" | custom-call | flops 8589934592 | bytes 8388608 | tf_op jit(solution)/shard_map/pallas_call | solution.py:389
  145.2 1.1 copy.12
  (4 shorter events, 0.1 us)
Async XLA Ops:
  0.0 2.3 %copy-start = (bf16[48,128,128]{2,1,0:T(8,128)(2,1)S(1)}, bf16[48,128,128]{2,1,0:T(8,128)(2,1)}, u32[]{:S(2)}) copy-start(bf16[48,128,128]{2,1,0:T(8,128)(2,1)} %param.5) | copy-start | bytes 4718596
  2.3 2.2 %copy-start.1 = (bf16[1,2048,8,128]{3,2,1,0:T(8,128)(2,1)S(1)}, bf16[1,2048,8,128]{3,2,1,0:T(8,128)(2,1)}, u32[]{:S(2)}) copy-start(bf16[1,2048,8,128]{3,2,1,0:T(8,128)(2,1)} %param.4) | copy-start | bytes 12582916

commit v6 on v5

--- a/solution.py
+++ b/solution.py
@@ -19,8 +19,8 @@
 
 def cycle_kernel(
     nz, nx, factor_ref, send_ref, meta_ref, place_ref, out_ref, f_ref, got_ref, picks_ref, bsend,
-    bgot, w_ref, wall, sibtx, sibrx, part, ytx1, yrx1, ytx2, yrx2, ztx, zrx, zg, xt, ptx, prx, relay,
-    acc, s_m, r_m, s_a, r_a, s_b, r_b, s_j, r_j, s_w, r_w, s_sib, r_sib, s_y1, r_y1, s_y2, r_y2,
+    bgot, w_ref, wall, sibtx, sibrx, part, ytx, yrx, ztx, zrx, zg, xt, ptx, prx, relay,
+    acc, s_m, r_m, s_a, r_a, s_b, r_b, s_j, r_j, s_w, r_w, s_sib, r_sib, s_y, r_y,
     s_z, r_z, s_gz, r_gz, s_gy, r_gy, s_gs, r_gs, s_p, r_p,
 ):
     pair, aux = lax.axis_index("pair"), lax.axis_index("aux")
@@ -176,29 +176,19 @@
             return carry
 
         lax.fori_loop(0, NY, block, 0)
-        ytx1[t] = part[t, lax.rem(y + 2, NY)].astype(BF16)
-        go(ytx1.at[t, :mid], yrx1.at[t, 0], s_y1.at[t, 0], r_y1.at[t, 0], up)
-        go(ytx1.at[t, mid:], yrx1.at[t, 1], s_y1.at[t, 1], r_y1.at[t, 1], down)
-
-    def y_relay_sum(t):
-        above, below = lax.rem(y + 1, NY), lax.rem(y + NY - 1, NY)
-        landed(yrx1.at[t, 0], r_y1.at[t, 0])
-        ytx2[t, 0, :mid] = (part[t, above, :mid] + yrx1[t, 0].astype(F32)).astype(BF16)
-        ytx2[t, 0, mid:] = part[t, above, mid:].astype(BF16)
-        go(ytx2.at[t, 0], yrx2.at[t, 0], s_y2.at[t, 0], r_y2.at[t, 0], up)
-        landed(yrx1.at[t, 1], r_y1.at[t, 1])
-        ytx2[t, 1, :mid] = part[t, below, :mid].astype(BF16)
-        ytx2[t, 1, mid:] = (part[t, below, mid:] + yrx1[t, 1].astype(F32)).astype(BF16)
-        go(ytx2.at[t, 1], yrx2.at[t, 1], s_y2.at[t, 1], r_y2.at[t, 1], down)
+        for d in (2, 1, 3):
+            ytx[t, d] = part[t, lax.rem(y + d, NY)].astype(BF16)
+            go(ytx.at[t, d], yrx.at[t, d], s_y.at[t, d], r_y.at[t, d], at(y + d, z, core))
 
     def z_copy(t, d):
         to = lax.rem(z + d, nz)
         return copy(ztx.at[t, to], zrx.at[t, d], s_z.at[t], r_z.at[t], at(y, z + d, core))
 
     def y_sum(t):
-        landed(yrx2.at[t, 0], r_y2.at[t, 0])
-        landed(yrx2.at[t, 1], r_y2.at[t, 1])
-        total = part[t, y] + yrx2[t, 0].astype(F32) + yrx2[t, 1].astype(F32)
+        total = part[t, y]
+        for d in (1, 3, 2):
+            landed(yrx.at[t, d], r_y.at[t, d])
+            total = total + yrx[t, d].astype(F32)
         ztx[t] = total.reshape(nz, seg, cols).astype(BF16)
 
         def send(d, carry):
@@ -235,26 +225,15 @@
         joined = zg[t].astype(F32).reshape(half, cols).astype(BF16)
         xt[t, y, pl.ds(pl.multiple_of(core * half, half), half), :] = joined
         mine = half_of(t, y, 0, half)
-        go(mine, mine, s_gy.at[t, 0], r_gy.at[t, 0], up)
-        go(mine, mine, s_gy.at[t, 1], r_gy.at[t, 1], down)
+        for d in (2, 1, 3):
+            go(mine, mine, s_gy.at[t, d], r_gy.at[t, d], at(y + d, z, core))
         go(mine, mine, s_gs.at[t, 0], r_gs.at[t, 0], sib)
 
     def y_gather(t):
-        landed(half_of(t, y - 1, 0, half), r_gy.at[t, 0])
-        piece = half_of(t, y - 1, 0, mid)
-        go(piece, piece, s_gy.at[t, 2], r_gy.at[t, 2], up)
-        landed(half_of(t, y + 1, 0, half), r_gy.at[t, 1])
-        piece = half_of(t, y + 1, mid, mid)
-        go(piece, piece, s_gy.at[t, 3], r_gy.at[t, 3], down)
-        for k, d in ((1, -1), (2, 1)):
-            piece = half_of(t, y + d, 0, half)
-            go(piece, piece, s_gs.at[t, k], r_gs.at[t, k], sib)
-
-    def y_relay_gather(t):
-        landed(half_of(t, y + 2, 0, mid), r_gy.at[t, 2])
-        landed(half_of(t, y + 2, mid, mid), r_gy.at[t, 3])
-        piece = half_of(t, y + 2, 0, half)
-        go(piece, piece, s_gs.at[t, 3], r_gs.at[t, 3], sib)
+        for d in (1, 3, 2):
+            piece = half_of(t, y - d, 0, half)
+            landed(piece, r_gy.at[t, d])
+            go(piece, piece, s_gs.at[t, d], r_gs.at[t, d], sib)
 
     def block_product(t):
         for k in range(4):
@@ -292,7 +271,7 @@
             go(ptx.at[2, high], relay.at[h, 1], s_p.at[h, 3], r_p.at[h, 3], left)
 
     stages = (
-        weights_product, core_sum, y_relay_sum, y_sum, z_sum, z_gather, y_gather, y_relay_gather, block_product,
+        weights_product, core_sum, y_sum, z_sum, z_gather, y_gather, block_product,
     )
     def give_back(h):
         piece = slice(h * rows, (h + 1) * rows)
@@ -318,7 +297,7 @@
         if step == 3:
             landed(got_ref.at[1, : n - 1], r_a.at[1])
             combine(1)
-        if step == 14:
+        if step == 12:
             give_back(0)
         for k in reversed(range(len(stages))):
             if 0 <= step - k < chunks:
@@ -383,7 +362,7 @@
     dma = pltpu.SemaphoreType.DMA
     vmem = pl.BlockSpec(memory_space=pltpu.VMEM)
     pairs = [
-        (1,), (2,), (2,), (2, 6), (2, 4), (chunks,), (chunks, 2), (chunks, 2), (chunks,), (chunks,),
+        (1,), (2,), (2,), (2, 6), (2, 4), (chunks,), (chunks, NY), (chunks,), (chunks,),
         (chunks, 4), (chunks, 4), (2, 6),
     ]
     return pl.pallas_call(
@@ -402,10 +381,8 @@
             pltpu.VMEM((chunks, NY, half, cols), F32),
             pltpu.VMEM((chunks, NY, half, cols), F32),
             pltpu.VMEM((chunks, NY, half, cols), F32),
-            pltpu.VMEM((chunks, half, cols), BF16),
-            pltpu.VMEM((chunks, 2, mid, cols), BF16),
-            pltpu.VMEM((chunks, 2, half, cols), BF16),
-            pltpu.VMEM((chunks, 2, half, cols), BF16),
+            pltpu.VMEM((chunks, NY, half, cols), BF16),
+            pltpu.VMEM((chunks, NY, half, cols), BF16),
             pltpu.VMEM((chunks, nz, seg, cols), BF16),
             pltpu.VMEM((chunks, nz, seg, cols), BF16),
             pltpu.VMEM((chunks, nz, seg, cols), BF16),

time: 146 us -> 140 us (0.959)
  Pallas kernels: 141 us -> 134 us
    pallas_call x1, Pallas kernels: 141 us -> 134 us  [cycle(): pl.pallas_call(functools.partial(cycle_kernel, nz, nx), out_shape=jax.Sha...]
where the time goes in v6:
time: 140 us
  Pallas kernels  134 us (96%)
  local copies, waits for them, and re-layouts  2.77 us (2%)
  other arithmetic  1.96 us (1%)
    pallas_call x1, Pallas kernels, cycle(): pl.pallas_call(functools.partial(cycle_kernel, nz, nx), out_shape=jax.Sha...  134 us

profile of v6, /device:TPU:1, one launch (start us, length us, event | category | flops | bytes accessed | tf_op | source)
XLA Modules:
  0.0 140.1 jit_solution(8638141221671888456)
XLA Ops:
  0.0 0.0 copy-start
  0.0 0.8 add_bitcast_fusion
  0.8 0.8 select_reduce_fusion
  1.7 0.2 convert_reduce_fusion
  1.9 0.1 fusion.4
  2.0 0.3 fusion.5
  2.3 0.0 copy-done
  2.3 0.0 copy-start.1
  2.3 0.5 fusion
  2.9 0.2 copy.6
  3.1 1.3 copy-done.1
  4.5 134.4 %shard_map.46 = bf16[48,128,128]{2,1,0:T(8,128)(2,1)S(1)} custom-call(bf16[2048,8,128]{2,1,0:T(8,128)(2,1)S(1)} %bitcast.15, bf16[64,2,32,128]{3,2,1,0:T(8,128)(2,1)S(1)} %bitcast.14, f32[64,2,128]{2,1,0:T(2,128)S(1)} %bitcast.16, bf16[2,48,64]{2,1,0:T(8,128)(2,1)S(1)} %add_convert_fusion.place_ref), custom_call_target="tpu_custom_call" | custom-call | flops 8589934592 | bytes 8388608 | tf_op jit(solution)/shard_map/pallas_call | solution.py:368
  138.9 1.1 copy.12
  (4 shorter events, 0.1 us)
Async XLA Ops:
  0.0 2.3 %copy-start = (bf16[48,128,128]{2,1,0:T(8,128)(2,1)S(1)}, bf16[48,128,128]{2,1,0:T(8,128)(2,1)}, u32[]{:S(2)}) copy-start(bf16[48,128,128]{2,1,0:T(8,128)(2,1)} %param.5) | copy-start | bytes 4718596
  2.3 2.2 %copy-start.1 = (bf16[1,2048,8,128]{3,2,1,0:T(8,128)(2,1)S(1)}, bf16[1,2048,8,128]{3,2,1,0:T(8,128)(2,1)}, u32[]{:S(2)}) copy-start(bf16[1,2048,8,128]{3,2,1,0:T(8,128)(2,1)} %param.4) | copy-start | bytes 12582916

commit v7 on v6

--- a/solution.py
+++ b/solution.py
@@ -19,7 +19,7 @@
 
 def cycle_kernel(
     nz, nx, factor_ref, send_ref, meta_ref, place_ref, out_ref, f_ref, got_ref, picks_ref, bsend,
-    bgot, w_ref, wall, sibtx, sibrx, part, ytx, yrx, ztx, zrx, zg, xt, ptx, prx, relay,
+    bgot, w_ref, wall, sibtx, sibrx, part, ytx, yrx, ztx, zrx, zg, xt, ptx, prx,
     acc, s_m, r_m, s_a, r_a, s_b, r_b, s_j, r_j, s_w, r_w, s_sib, r_sib, s_y, r_y,
     s_z, r_z, s_gz, r_gz, s_gy, r_gy, s_gs, r_gs, s_p, r_p,
 ):
@@ -38,6 +38,7 @@
     sib = at(y, z, 1 - core)
     up, down = at(y + 1, z, core), at(y - 1, z, core)
     right, left = {"aux": lax.rem(aux + 1, nx)}, {"aux": lax.rem(aux + nx - 1, nx)}
+    across = {"aux": lax.rem(aux + 2, nx)}
 
     def copy(src, dst, send, recv, to):
         return pltpu.make_async_remote_copy(
@@ -46,7 +47,7 @@
 
     n = 2 * NY * nz
     barrier = pltpu.get_barrier_semaphore()
-    for peer in (right, left):
+    for peer in (right, left, across):
         pl.semaphore_signal(barrier, inc=1, device_id=peer, device_id_type=MESH)
 
     def peer_at(d):
@@ -59,7 +60,7 @@
         return carry
 
     lax.fori_loop(1, n, greet, 0)
-    pl.semaphore_wait(barrier, n + 1)
+    pl.semaphore_wait(barrier, n + 2)
 
     sent = []
 
@@ -251,13 +252,6 @@
             acc[k] = jnp.where(b == 0, got, acc[k] + got)
             return carry
 
-        if t and ORDER[t - 1][0] == 2:
-            g = ORDER[t - 1][1]
-            low, high = slice(g * rows, g * rows + half), slice(g * rows + half, (g + 1) * rows)
-            landed(relay.at[g, 0], r_p.at[g, 2])
-            go(relay.at[g, 0], prx.at[2, low], s_p.at[g, 4], r_p.at[g, 4], right)
-            landed(relay.at[g, 1], r_p.at[g, 3])
-            go(relay.at[g, 1], prx.at[2, high], s_p.at[g, 5], r_p.at[g, 5], left)
         lax.fori_loop(0, NY, block, 0)
         if share < 3:
             ptx[share, piece] = acc[0].astype(BF16)
@@ -266,17 +260,15 @@
         if share == 1:
             go(ptx.at[1, piece], prx.at[0, piece], s_p.at[h, 0], r_p.at[h, 0], right)
         if share == 2:
-            low, high = slice(h * rows, h * rows + half), slice(h * rows + half, (h + 1) * rows)
-            go(ptx.at[2, low], relay.at[h, 0], s_p.at[h, 2], r_p.at[h, 2], right)
-            go(ptx.at[2, high], relay.at[h, 1], s_p.at[h, 3], r_p.at[h, 3], left)
+            go(ptx.at[2, piece], prx.at[2, piece], s_p.at[h, 2], r_p.at[h, 2], across)
 
     stages = (
         weights_product, core_sum, y_sum, z_sum, z_gather, y_gather, block_product,
     )
     def give_back(h):
         piece = slice(h * rows, (h + 1) * rows)
-        for k in (0, 1, 4, 5):
-            landed(prx.at[min(k, 2), piece if k < 2 else slice(half)], r_p.at[h, k])
+        for k in range(3):
+            landed(prx.at[k, piece], r_p.at[h, k])
         total = acc[1 + h]
         for source in range(3):
             total = total + prx[source, piece].astype(F32)
@@ -305,11 +297,10 @@
     give_back(1)
 
     count = out_ref.shape[0]
-    few = count // 2
-
-    def spot(who, h, first_block):
+
+    def spot(who, h):
         low = lax.rem(who + nx, nx) * (2 * thin) + h * thin
-        return out_ref.at[pl.ds(first_block, few), pl.ds(pl.multiple_of(low, thin), thin), :]
+        return out_ref.at[:, pl.ds(pl.multiple_of(low, thin), thin), :]
 
     for h in range(2):
         landed(bgot.at[h, : n - 1], r_b.at[h])
@@ -319,22 +310,12 @@
             total = total + jnp.dot(place_ref[r], rows_r, preferred_element_type=F32)
         low = pl.multiple_of(aux * (2 * thin) + h * thin, thin)
         out_ref[:, pl.ds(low, thin), :] = total.reshape(count, thin, width).astype(BF16)
-        for q, to in enumerate((right, left)):
-            for b in range(2):
-                mine = spot(aux, h, (b ^ q) * few)
-                m = 2 * q + b
-                go(mine, mine, s_j.at[h, m], r_j.at[h, m], to)
+        mine = spot(aux, h)
+        for k, to in enumerate((across, right, left)):
+            go(mine, mine, s_j.at[h, k], r_j.at[h, k], to)
     for h in range(2):
-        from_left, from_right = spot(aux - 1, h, 0), spot(aux + 1, h, few)
-        landed(from_left, r_j.at[h, 0])
-        go(from_left, from_left, s_j.at[h, 4], r_j.at[h, 4], right)
-        landed(from_right, r_j.at[h, 2])
-        go(from_right, from_right, s_j.at[h, 5], r_j.at[h, 5], left)
-    for h in range(2):
-        landed(spot(aux - 1, h, few), r_j.at[h, 1])
-        landed(spot(aux + 1, h, 0), r_j.at[h, 3])
-        landed(spot(aux + 2, h, 0), r_j.at[h, 4])
-        landed(spot(aux + 2, h, few), r_j.at[h, 5])
+        for k, d in enumerate((2, -1, 1)):
+            landed(spot(aux + d, h), r_j.at[h, k])
 
     def left_here(src, send):
         copy(src, src, send, send, sib).wait_send()
@@ -362,8 +343,8 @@
     dma = pltpu.SemaphoreType.DMA
     vmem = pl.BlockSpec(memory_space=pltpu.VMEM)
     pairs = [
-        (1,), (2,), (2,), (2, 6), (2, 4), (chunks,), (chunks, NY), (chunks,), (chunks,),
-        (chunks, 4), (chunks, 4), (2, 6),
+        (1,), (2,), (2,), (2, 3), (2, 4), (chunks,), (chunks, NY), (chunks,), (chunks,),
+        (chunks, 4), (chunks, 4), (2, 3),
     ]
     return pl.pallas_call(
         functools.partial(cycle_kernel, nz, nx),
@@ -389,7 +370,6 @@
             pltpu.VMEM((chunks, NY, 2 * half, cols), BF16),
             pltpu.VMEM((3, rows, flat), BF16),
             pltpu.VMEM((3, rows, flat), BF16),
-            pltpu.VMEM((2, 2, half, flat), BF16),
             pltpu.VMEM((3, 2 * half, flat), F32),
         ]
         + [dma(shape) for shape in pairs for _ in range(2)],

time: 140 us -> 139 us (level)
  no operation moved by 1% of the time
where the time goes in v7:
time: 139 us
  Pallas kernels  133 us (96%)
  local copies, waits for them, and re-layouts  2.77 us (2%)
  other arithmetic  1.96 us (1%)
    pallas_call x1, Pallas kernels, cycle(): pl.pallas_call(functools.partial(cycle_kernel, nz, nx), out_shape=jax.Sha...  133 us

profile of v7, /device:TPU:1, one launch (start us, length us, event | category | flops | bytes accessed | tf_op | source)
XLA Modules:
  0.0 138.9 jit_solution(3163239082834332343)
XLA Ops:
  0.0 0.0 copy-start
  0.0 0.8 add_bitcast_fusion
  0.8 0.8 select_reduce_fusion
  1.7 0.2 convert_reduce_fusion
  1.9 0.1 fusion.4
  2.0 0.3 fusion.5
  2.3 0.0 copy-done
  2.3 0.0 copy-start.1
  2.3 0.5 fusion
  2.9 0.2 copy.6
  3.1 1.3 copy-done.1
  4.5 133.3 %shard_map.46 = bf16[48,128,128]{2,1,0:T(8,128)(2,1)S(1)} custom-call(bf16[2048,8,128]{2,1,0:T(8,128)(2,1)S(1)} %bitcast.15, bf16[64,2,32,128]{3,2,1,0:T(8,128)(2,1)S(1)} %bitcast.14, f32[64,2,128]{2,1,0:T(2,128)S(1)} %bitcast.16, bf16[2,48,64]{2,1,0:T(8,128)(2,1)S(1)} %add_convert_fusion.place_ref), custom_call_target="tpu_custom_call" | custom-call | flops 8589934592 | bytes 8388608 | tf_op jit(solution)/shard_map/pallas_call | solution.py:349
  137.8 1.1 copy.12
  (4 shorter events, 0.1 us)
Async XLA Ops:
  0.0 2.3 %copy-start = (bf16[48,128,128]{2,1,0:T(8,128)(2,1)S(1)}, bf16[48,128,128]{2,1,0:T(8,128)(2,1)}, u32[]{:S(2)}) copy-start(bf16[48,128,128]{2,1,0:T(8,128)(2,1)} %param.5) | copy-start | bytes 4718596
  2.3 2.2 %copy-start.1 = (bf16[1,2048,8,128]{3,2,1,0:T(8,128)(2,1)S(1)}, bf16[1,2048,8,128]{3,2,1,0:T(8,128)(2,1)}, u32[]{:S(2)}) copy-start(bf16[1,2048,8,128]{3,2,1,0:T(8,128)(2,1)} %param.4) | copy-start | bytes 12582916
